TPU v7x, 512 devices: a whole 4x8x8 slice. The times are simulated.
512 devices in a mesh: scen: 32 (over z, y_lo, core), col: 16 (over x, y_hi).
Axes of the slice: x: 4, y: 8 (y_hi: 4, y_lo: 2; y = y_hi * 2 + y_lo), z: 8, core: 2. Of those that a mesh axis runs over, the one named last changes fastest.
Arguments:
- inverse_factor: bfloat16 [512, 512, 512], P(('scen', 'col')), as said below
- true_orders: int32 [512], P(('scen', 'col')), may hold values from 64 to 512, as said below
- slab_border: bfloat16 [512, 256, 512], P(('scen', 'col')), may hold values from -0.25 to 0.25
- slab_columns: int32 [512, 256], P('scen'), may hold values from 0 to 511
- panel_border: bfloat16 [16, 512, 48, 512], P('col', 'scen'), may hold values from -6 to 6
- panel_rows: int32 [16, 512, 48], P('col', 'scen'), may hold values from 0 to 479
- barrier_diag: float32 [512], replicated, may hold values from 20 to 400
Outputs:
- diag_factor: float32 [512, 512], P('col')
- panel_factor: float32 [7680, 512], P(('scen', 'col'))
Inputs may be any that keep to these rules, and one draw needn't show every extreme that they name: `inverse_factor`: symmetric; its leading block of each scenario's true order is positive definite. `true_orders`: scenario 0 has the full padded order.
All inputs are finite; a program needn't handle non-finite values.
Results may differ from a plain program's by a relative error of at most 0.0003.
The roundings to bfloat16 on the way count: a program that leaves them out, or rounds other values in their place, can miss the bound.
Values may be sent and summed in bfloat16 or wider, within the bound.
A program may use at most 64 MiB of HBM per device.

v0:
```python
import jax
import jax.numpy as jnp
from jax import lax
from jax.sharding import PartitionSpec as P

NF = 8192
DIAG = 512


highest = lax.Precision.HIGHEST


def masked_product(factor, order_value, border):
    positions = jnp.arange(factor.shape[0], dtype=jnp.int32)
    inside = positions < order_value
    masked = jnp.where(inside[:, None] & inside[None, :], factor, jnp.zeros((), jnp.bfloat16))
    return jnp.dot(border, masked, preferred_element_type=jnp.float32)


def spread_map(index, width):
    return (index[:, None] == jnp.arange(width, dtype=jnp.int32)[None, :]).astype(jnp.float32)


def place_panel(running, coupling, row_index, columns):
    widened = jnp.dot(coupling, spread_map(columns, running.shape[1]), precision=highest)
    row_map = spread_map(row_index, running.shape[0])
    return running + jnp.einsum("br,bd->rd", row_map, widened, precision=highest)


def diag_step(running, operands):
    border, moved_rows, columns = operands
    terms = jnp.einsum("ap,bp->ab", border, moved_rows, preferred_element_type=jnp.float32)
    col_map = spread_map(columns, running.shape[0])
    widened = jnp.dot(terms, col_map, precision=highest)
    return (running + jnp.einsum("ad,ae->de", col_map, widened, precision=highest), None)


def panel_step(running, operands):
    border_values, moved_rows, row_index, columns = operands
    coupling = jnp.einsum(
        "bp,jp->bj", border_values, moved_rows, preferred_element_type=jnp.float32
    )
    return (place_panel(running, coupling, row_index, columns), None)


def shards(
    inverse_factor, true_orders, slab_border, slab_columns, panel_border, panel_rows, barrier_diag
):
    local_count = inverse_factor.shape[0]
    col_count = lax.axis_size("col")
    col_place = lax.axis_index("col")
    product = masked_product(inverse_factor[0], true_orders[0], slab_border[0])
    results = [product.astype(jnp.bfloat16)]
    transformed = jnp.stack(results)
    own_columns = lax.dynamic_slice_in_dim(slab_columns, col_place * local_count, local_count, 0)
    zero_diag = jnp.zeros((DIAG, DIAG), jnp.float32)
    diag_partial, _ = lax.scan(diag_step, zero_diag, (slab_border, transformed, own_columns))
    schur_diag = lax.psum(diag_partial, ("scen", "col")) + jnp.diag(barrier_diag)
    factor_full = jnp.linalg.cholesky(schur_diag)
    rows_panel = (NF - DIAG) // col_count
    zero_panel = jnp.zeros((rows_panel, DIAG), jnp.float32)
    group_border = panel_border[0]
    group_rows = panel_rows[0]
    total, _ = lax.scan(
        panel_step,
        zero_panel,
        (
            group_border,
            lax.all_gather(transformed, "col", axis=0, tiled=True),
            group_rows,
            slab_columns,
        ),
    )
    own_rows = lax.psum_scatter(total, "scen", scatter_dimension=0, tiled=True)
    solved = lax.linalg.triangular_solve(
        factor_full, own_rows, left_side=False, lower=True, transpose_a=True
    )
    diag_rows = DIAG // col_count
    return (lax.dynamic_slice_in_dim(factor_full, col_place * diag_rows, diag_rows, 0), solved)


def solution(mesh):
    in_specs = (
        P(("scen", "col"), None, None),
        P(("scen", "col")),
        P(("scen", "col"), None, None),
        P("scen", None),
        P("col", "scen", None, None),
        P("col", "scen", None),
        P(),
    )
    out_specs = (P("col", None), P(("scen", "col"), None))
    return jax.shard_map(shards, mesh=mesh, in_specs=in_specs, out_specs=out_specs, check_vma=False)
```

profile of v0, /device:TPU:1, one launch (start us, length us, event | category | flops | bytes accessed | tf_op | source)
XLA Modules:
  0.0 737.0 jit_solution(13014186452016274001)
XLA Ops:
  9.0 1.5 convolution_convert_fusion
  12.0 1.7 fusion.14
  14.4 1.3 dynamic-slice.4
  16.3 311.6 %all-reduce.5.cloned.1.call-done = f32[512,512]{0,1:T(8,128)} async-done(((f32[512,512]{0,1:T(8,128)}), f32[512,512]{0,1:T(8,128)}) %all-reduce.5.cloned.1.call-update) | async-done | bytes 1048592 | tf_op jit(solution)/shard_map/psum | solution.py:58
  328.0 1.4 select_add_fusion
  329.4 1.4 copy.22
  330.8 1.4 fusion.10
  332.2 11.7 %cholesky.103 = f32[128,128]{1,0:T(8,128)S(1)} custom-call(f32[128,128]{1,0:T(8,128)S(1)} %cholesky.263), custom_call_target="Cholesky" | custom-call | tf_op jit(solution)/shard_map/jit(cholesky)/cholesky | solution.py:59
  344.7 9.8 %custom-call.30 = f32[1,128,128]{1,2,0:T(8,128)S(1)} custom-call(f32[1,128,128]{2,1,0:T(8,128)S(1)} %get-tuple-element.132), custom_call_target="InvertDiagBlocksLowerTriangular" | custom-call | tf_op jit(solution)/shard_map/jit(cholesky)/cholesky | solution.py:59
  355.3 11.7 %cholesky.215 = f32[128,128]{1,0:T(8,128)S(1)} custom-call(f32[128,128]{1,0:T(8,128)S(1)} %cholesky.267), custom_call_target="Cholesky" | custom-call | tf_op jit(solution)/shard_map/jit(cholesky)/cholesky | solution.py:59
  367.8 10.6 %custom-call.31 = f32[1,128,128]{1,2,0:T(8,128)} custom-call(f32[1,128,128]{2,1,0:T(8,128)S(1)} %get-tuple-element.130), custom_call_target="InvertDiagBlocksLowerTriangular" | custom-call | tf_op jit(solution)/shard_map/jit(cholesky)/cholesky | solution.py:59
  380.2 1.2 convolution_dynamic-update-slice_fusion
  382.1 12.3 %cholesky.236 = f32[128,128]{1,0:T(8,128)} custom-call(f32[128,128]{1,0:T(8,128)S(1)} %cholesky.272), custom_call_target="Cholesky" | custom-call | tf_op jit(solution)/shard_map/jit(cholesky)/cholesky | solution.py:59
  395.3 1.5 select_reduce_fusion.1
  396.8 11.3 %custom-call.32 = f32[1,128,128]{1,2,0:T(8,128)} custom-call(f32[1,128,128]{2,1,0:T(8,128)} %get-tuple-element.128), custom_call_target="InvertDiagBlocksLowerTriangular" | custom-call | tf_op jit(solution)/shard_map/jit(cholesky)/cholesky | solution.py:59
  409.7 11.9 %cholesky.253 = f32[128,128]{1,0:T(8,128)S(1)} custom-call(f32[128,128]{1,0:T(8,128)S(1)} %convolution_subtract_fusion.2), custom_call_target="Cholesky" | custom-call | tf_op jit(solution)/shard_map/jit(cholesky)/cholesky | solution.py:59
  427.5 6.5 copy.36
  434.0 61.8 %while.17 = (s32[]{:T(128)}, f32[480,512]{1,0:T(8,128)S(1)}, s32[16,48]{1,0:T(8,128)}, bf16[16,48,512]{2,1,0:T(8,128)(2,1)}, bf16[16,256,512]{2,1,0:T(8,128)(2,1)}, /*index=5*/s32[16,256]{1,0:T(8,128)}, s32[]{:T(128)}, s32[]{:T(128)}) while((s32[]{:T(128)}, f32[480,512]{1,0:T(8,128)S(1)}, s32[16,48]{1,0:T(8,128)}, ...), condition=%wide.region_10.11_spmd.clone, body=%wide.region_9.10_spmd.clone.sunk | while | flops 230283776 | bytes 2577071 | solution.py:64
  435.4 1.2 fusion.79
  439.3 1.2 fusion.79
  447.0 1.2 fusion.79
  450.9 1.2 fusion.79
  454.7 1.2 fusion.79
  458.6 1.2 fusion.79
  470.2 1.2 fusion.79
  496.9 10.9 %while.16 = (s32[]{:T(128)}, f32[512,512]{0,1:T(8,128)S(1)}, s32[4,2]{0,1:T(2,128)S(1)}, f32[4,128,128]{2,1,0:T(8,128)}, s32[]{:T(128)}) while((s32[]{:T(128)}, f32[512,512]{0,1:T(8,128)S(1)}, s32[4,2]{0,1:T(2,128)S(1)}, f32[4,128,128]{2,1,0:T(8,128)}, s32[]{:T(128)}) %tuple.53), condition=%wide.while_cond, body=%wide.while_body.sunk | while | flops 2 | bytes 393329 | solution.py:75
  497.5 1.4 dynamic-slice.19
  500.2 1.4 dynamic-slice.19
  502.9 1.4 dynamic-slice.19
  505.6 1.4 dynamic-slice.19
  507.7 40.1 %custom-call.33 = f32[4,128,128]{1,2,0:T(8,128)S(1)} custom-call(f32[4,128,128]{2,1,0:T(8,128)} %get-tuple-element.57), custom_call_target="InvertDiagBlocksLowerTriangular" | custom-call | tf_op jit(solution)/shard_map/triangular_solve | solution.py:75
  547.9 176.8 %all-reduce.7.cloned.1.call-done = f32[480,512]{1,0:T(8,128)} async-done(((f32[480,512]{1,0:T(8,128)}), f32[480,512]{1,0:T(8,128)}) %all-reduce.7.cloned.1.call-update) | async-done | bytes 983056
  (151 shorter events, 76.9 us)
Async XLA Ops:
  8.0 1.0 copy-start
  8.0 320.0 %copy-start.5 = (f32[512]{0:T(512)S(1)}, f32[512]{0:T(512)}, u32[]{:S(2)}) copy-start(f32[512]{0:T(512)} %param.15) | copy-start | bytes 6148
  8.0 319.9 %all-reduce.5.cloned.1.call-start = ((), (), s32[]{:S(2)}) async-start(), calls=%async_computation | async-start | bytes 2097152 | tf_op jit(solution)/shard_map/psum | solution.py:58
  10.5 3.3 copy-start.3
  13.7 413.7 %all-gather.3.cloned.1.call-start = ((), (), s32[]{:S(2)}) async-start(), calls=%async_computation.1 | async-start | bytes 4456448 | tf_op jit(solution)/shard_map/all_gather | solution.py:69
  14.3 710.4 %all-reduce.7.cloned.1.call-start = ((), (), s32[]{:S(2)}) async-start(), calls=%async_computation.2 | async-start | bytes 1966080
  328.0 2.8 copy-start.2
  355.3 12.5 %copy-start.4 = (f32[384,128]{1,0:T(8,128)}, f32[384,128]{1,0:T(8,128)S(1)}, u32[]{:S(2)}) copy-start(f32[384,128]{1,0:T(8,128)S(1)} %convolution_subtract_fusion) | copy-start | bytes 589828
  495.8 1.0 copy-start.1
Sparse Core Ops, SparseCore 0:
  13.9 314.0 all-reduce.4
Sparse Core Ops, SparseCore 1:
  17.2 90.6 all-gather.2
  496.9 227.7 all-reduce.6
where the time goes:
time: 740 us; the launch traced here: 737 us
  waiting for transfers between devices  489 us (66%)
  other arithmetic  127 us (17%)
  matrix products  51 us (7%)
  local copies, waits for them, and re-layouts  49.6 us (7%)
  between operations  19.7 us (3%)
    psum x1, waiting for transfers between devices, shards(): lax.psum(diag_partial, ('scen', 'col')) + jnp.diag(barrier_diag)  312 us
    unnamed x4, waiting for transfers between devices  177 us
    another operation x14, other arithmetic, shards(): factor_full = jnp.linalg.cholesky(schur_diag)  82.8 us
    another operation x4, other arithmetic, shards(): lax.linalg.triangular_solve(factor_full, own_rows, left_side=False, lower...  41 us
    dot_general x16, matrix products, panel_step(): jnp.einsum('bp,jp->bj', border_values, moved_rows, preferred_element_type...  18.7 us
  transfers between devices with their start and end apart: 3, of which 2 were waited for; matrix products, arithmetic and copies ran while one was open for 20% of the time, Pallas kernels for 0%

commit v1 on v0

v1 whole, which is shorter than its diff:
```python
import functools

import jax
import jax.numpy as jnp
from jax import lax
from jax.experimental import pallas as pl
from jax.experimental.pallas import tpu as pltpu
from jax.sharding import PartitionSpec as P

HIGHEST = lax.Precision.HIGHEST
MESH = pl.DeviceIdType.MESH
F32 = jnp.float32
BF16 = jnp.bfloat16
DIAG = 512
NB = DIAG // 128
BLOCKS = [(r, j) for r in range(NB) for j in range(r, NB)]
TILES = 16 * len(BLOCKS)


def split(value, parts):
    out = []
    for _ in range(parts - 1):
        piece = value.astype(BF16)
        out.append(piece)
        value = value - piece.astype(F32)
    return out + [value.astype(BF16)]


def dot(a, b, ca, cb, precision=None):
    return lax.dot_general(
        a, b, (((ca,), (cb,)), ((), ())), precision=precision, preferred_element_type=F32
    )


def one_hot(targets, height):
    width = targets.shape[1]
    place = lax.broadcasted_iota(jnp.int32, (height, width), 0)
    return jnp.where(place == targets, 1.0, 0.0).astype(BF16)


class Wire:
    def __init__(self, send_sem, recv_sem):
        self.send_sem, self.recv_sem, self.used, self.sends = send_sem, recv_sem, 0, []

    def start(self, src, dst, scen, col):
        k = self.used
        self.used += 1
        copy = pltpu.make_async_remote_copy(
            src_ref=src,
            dst_ref=dst,
            send_sem=self.send_sem.at[k],
            recv_sem=self.recv_sem.at[k],
            device_id=(scen, col),
            device_id_type=MESH,
        )
        copy.start()
        self.sends.append(copy)
        return copy

    def drain(self):
        for copy in self.sends:
            copy.wait_send()


def exchange_kernel(
    n_x, n_y, n_zy,
    order_ref, inv_ref, border_ref, columns_ref, panel_ref, rows_ref,
    diag_ref, slab_ref,
    pb, tr, coup, coup_in, packed, c_buf, half, z_buf, y_own, y_buf, x_own, x_buf, full,
    maps, row_map, wide, total, pc_buf, p_half, pz_buf,
    send_sem, recv_sem, local_sem,
):
    scen, col = lax.axis_index("scen"), lax.axis_index("col")
    core, zy = scen % 2, scen // 2
    x, y = col // n_y, col % n_y
    sibling = scen + 1 - 2 * core
    n_tiles = TILES // 2
    chunk = n_tiles // n_zy
    p_rows = total.shape[0] // 2
    p_chunk = p_rows // n_zy
    wire = Wire(send_sem, recv_sem)

    barrier = pltpu.get_barrier_semaphore()
    zy_peers = [((zy + d) % n_zy) for d in range(1, n_zy)]
    y_peers = [((y + d) % n_y) for d in range(1, n_y)]
    x_peers = [((x + d) % n_x) for d in range(1, n_x)]
    greet = [(sibling, col)]
    greet += [(p * 2 + core, col) for p in zy_peers]
    greet += [(scen, x * n_y + p) for p in y_peers]
    greet += [(scen, p * n_y + y) for p in x_peers]
    for device in greet:
        pl.semaphore_signal(barrier, inc=1, device_id=device, device_id_type=MESH)
    pl.semaphore_wait(barrier, len(greet))

    pb_copies = [
        wire.start(panel_ref.at[0, pl.ds(p * n_y, n_y)], pb.at[:, x], scen, p * n_y + y)
        for p in x_peers
    ]
    own_pb = pltpu.make_async_copy(panel_ref.at[0, pl.ds(x * n_y, n_y)], pb.at[:, x], local_sem.at[0])
    own_pb.start()

    order = order_ref[0]
    p_size = inv_ref.shape[1]
    border = border_ref[0]
    lanes = lax.broadcasted_iota(jnp.int32, border.shape, 1)
    inside = lanes < order
    cut = jnp.where(inside, border.astype(F32), 0.0).astype(BF16)
    moved = dot(cut, inv_ref[0], 1, 0)
    moved = jnp.where(inside, moved, 0.0).astype(BF16)
    tr[y] = moved
    tr_copies = [wire.start(tr.at[y], tr.at[y], scen, x * n_y + p) for p in y_peers]

    terms = 0.5 * (dot(border, moved, 1, 1) + dot(moved, border, 1, 1))
    own_map = one_hot(columns_ref[pl.ds(col, 1), :], DIAG)
    spread = sum(dot(own_map, piece, 1, 0) for piece in split(terms, 3))
    pieces = split(spread, 3)
    base = 0
    for r in range(NB):
        rows = slice(128 * r, 128 * r + 128)
        strip = sum(dot(piece[rows], own_map[128 * r :], 1, 1) for piece in pieces)
        for j in range(r, NB):
            block = strip[:, 128 * (j - r) : 128 * (j - r + 1)]
            packed[base : base + 16] = block.reshape(16, 8, 128)
            base += 16

    c_copy = wire.start(packed.at[pl.ds((1 - core) * n_tiles, n_tiles)], c_buf, sibling, col)
    flat = rows_ref[...]
    rows_dev = 15
    owner = (flat * 4370) >> 16
    slot = (owner % 2) * p_rows + (owner // 2) * p_chunk + (flat - owner * rows_dev)
    row_map[...] = one_hot(slot, 2 * p_rows)
    c_copy.wait_recv()
    half[...] = packed[pl.ds(core * n_tiles, n_tiles)] + c_buf[...]

    z_copies = [
        wire.start(half.at[pl.ds(p * chunk, chunk)], z_buf.at[k], p * 2 + core, col)
        for k, p in enumerate(zy_peers)
    ]

    def build_map(i, carry):
        maps[i] = one_hot(columns_ref[pl.ds(i, 1), :], DIAG)
        return carry

    lax.fori_loop(0, maps.shape[0], build_map, 0)
    for copy in z_copies:
        copy.wait_recv()
    y_own[...] = half[pl.ds(zy * chunk, chunk)] + jnp.sum(z_buf[...], axis=0)
    y_copies = [
        wire.start(y_own, y_buf.at[k], scen, x * n_y + p) for k, p in enumerate(y_peers)
    ]
    for copy in y_copies:
        copy.wait_recv()
    x_own[...] = y_own[...] + jnp.sum(y_buf[...], axis=0)
    x_copies = [
        wire.start(x_own, x_buf.at[k], scen, p * n_y + y) for k, p in enumerate(x_peers)
    ]
    for copy in x_copies:
        copy.wait_recv()
    mine = pl.ds((core * n_zy + zy) * chunk, chunk)
    full[mine] = x_own[...] + jnp.sum(x_buf[...], axis=0)
    g_copies = [wire.start(full.at[mine], full.at[mine], p * 2 + core, col) for p in zy_peers]

    own_pb.wait()
    for copy in pb_copies:
        copy.wait_recv()
    for copy in tr_copies:
        copy.wait_recv()

    def couple(i, carry):
        stacked = pb[i].reshape(n_x * pb.shape[2], p_size)
        coup[i] = dot(stacked, tr[i], 1, 1).reshape(coup.shape[1:])
        return carry

    lax.fori_loop(0, n_y, couple, 0)
    own_coup = pltpu.make_async_copy(coup.at[:, x], coup_in.at[pl.ds(x * n_y, n_y)], local_sem.at[1])
    own_coup.start()
    q_copies = [
        wire.start(coup.at[:, p], coup_in.at[pl.ds(x * n_y, n_y)], scen, p * n_y + y)
        for p in x_peers
    ]

    for copy in g_copies:
        copy.wait_recv()
    side = pl.ds(core * n_tiles, n_tiles)
    h_copy = wire.start(full.at[side], full.at[side], sibling, col)
    own_coup.wait()
    for copy in q_copies:
        copy.wait_recv()

    n_b = coup.shape[2]

    def widen(i, carry):
        high, low = split(coup_in[i], 2)
        both = dot(jnp.concatenate([high, low], axis=0), maps[i], 1, 1)
        wide[pl.ds(i * n_b, n_b), :] = both[:n_b] + both[n_b:]
        return carry

    lax.fori_loop(0, maps.shape[0], widen, 0)
    high, low = split(wide[...], 2)
    total[...] = dot(row_map[...], high, 1, 0) + dot(row_map[...], low, 1, 0)
    pc_copy = wire.start(total.at[pl.ds((1 - core) * p_rows, p_rows)], pc_buf, sibling, col)
    pc_copy.wait_recv()
    p_half[...] = total[pl.ds(core * p_rows, p_rows)] + pc_buf[...]
    pz_copies = [
        wire.start(p_half.at[pl.ds(p * p_chunk, p_chunk)], pz_buf.at[k], p * 2 + core, col)
        for k, p in enumerate(zy_peers)
    ]
    h_copy.wait_recv()
    diag_ref[...] = full[...]
    for copy in pz_copies:
        copy.wait_recv()
    slab_ref[...] = p_half[pl.ds(zy * p_chunk, p_chunk)] + jnp.sum(pz_buf[...], axis=0)
    wire.drain()


def exchange(n_x, n_y, n_zy, order, inverse_factor, border, columns, panel_border, flat_rows):
    n_scen = columns.shape[0]
    cbj, p_size = border.shape[1:]
    cbp = panel_border.shape[2]
    chunk = TILES // 2 // n_zy
    p_rows = 16 * n_zy
    n_copies = 2 + 3 * (n_zy - 1) + 2 * (n_y - 1) + 3 * (n_x - 1) + 1
    tile = (8, 128)
    vmem = pl.BlockSpec(memory_space=pltpu.VMEM)
    return pl.pallas_call(
        functools.partial(exchange_kernel, n_x, n_y, n_zy),
        name="exchange",
        out_shape=(
            jax.ShapeDtypeStruct((TILES,) + tile, F32),
            jax.ShapeDtypeStruct((16, DIAG), F32),
        ),
        in_specs=[pl.BlockSpec(memory_space=pltpu.SMEM)] + [vmem] * 5,
        out_specs=[vmem] * 2,
        scratch_shapes=[
            pltpu.VMEM((n_y, n_x, cbp, p_size), BF16),
            pltpu.VMEM((n_y, cbj, p_size), BF16),
            pltpu.VMEM((n_y, n_x, cbp, cbj), F32),
            pltpu.VMEM((n_scen, cbp, cbj), F32),
            pltpu.VMEM((TILES,) + tile, F32),
            pltpu.VMEM((TILES // 2,) + tile, F32),
            pltpu.VMEM((TILES // 2,) + tile, F32),
            pltpu.VMEM((n_zy - 1, chunk) + tile, F32),
            pltpu.VMEM((chunk,) + tile, F32),
            pltpu.VMEM((n_y - 1, chunk) + tile, F32),
            pltpu.VMEM((chunk,) + tile, F32),
            pltpu.VMEM((n_x - 1, chunk) + tile, F32),
            pltpu.VMEM((TILES,) + tile, F32),
            pltpu.VMEM((n_scen, DIAG, cbj), BF16),
            pltpu.VMEM((2 * p_rows, n_scen * cbp), BF16),
            pltpu.VMEM((n_scen * cbp, DIAG), F32),
            pltpu.VMEM((2 * p_rows, DIAG), F32),
            pltpu.VMEM((p_rows, DIAG), F32),
            pltpu.VMEM((p_rows, DIAG), F32),
            pltpu.VMEM((n_zy - 1, 16, DIAG), F32),
            pltpu.SemaphoreType.DMA((n_copies,)),
            pltpu.SemaphoreType.DMA((n_copies,)),
            pltpu.SemaphoreType.DMA((2,)),
        ],
        compiler_params=pltpu.CompilerParams(collective_id=0, has_side_effects=True),
    )(order, inverse_factor, border, columns, panel_border, flat_rows)


def factor_block(block):
    groups = 16
    tile = (8, 128)
    lane = lax.broadcasted_iota(jnp.int32, tile, 1)
    sub = lax.broadcasted_iota(jnp.int32, tile, 0)
    left = [block[8 * q : 8 * q + 8, :] for q in range(groups)]
    right = [jnp.where(lane == sub + 8 * q, 1.0, 0.0).astype(F32) for q in range(groups)]
    upper, inverse = [], []

    def spread(row):
        return jnp.broadcast_to(row, tile)

    for p in range(groups):
        column = {
            q: [jnp.broadcast_to(left[q][:, 8 * p + m : 8 * p + m + 1], tile) for m in range(8)]
            for q in range(p, groups)
        }
        pivot = column[p]
        row_l, row_r = left[p], right[p]
        out_l, out_r = jnp.zeros(tile, F32), jnp.zeros(tile, F32)
        for t in range(4):
            m, k = 2 * t, 2 * t + 1
            a, b, c = spread(pivot[m][m : m + 1]), spread(pivot[k][m : m + 1]), spread(pivot[k][k : k + 1])
            det = a * c - b * b
            over = 1.0 / det
            ia, ib, ic = c * over, -(b * over), a * over
            for n in range(k + 1, 8):
                e, f = spread(pivot[n][m : m + 1]), spread(pivot[n][k : k + 1])
                g, h = ia * e + ib * f, ib * e + ic * f
                for q in range(p, groups):
                    column[q][n] = column[q][n] - (column[q][m] * g + column[q][k] * h)
            lm, lk = spread(row_l[m : m + 1]), spread(row_l[k : k + 1])
            rm, rk = spread(row_r[m : m + 1]), spread(row_r[k : k + 1])
            l0, l1 = ia * lm + ib * lk, ib * lm + ic * lk
            r0, r1 = ia * rm + ib * rk, ib * rm + ic * rk
            if k < 7:
                cm = jnp.where(sub > k, pivot[m], 0.0)
                ck = jnp.where(sub > k, pivot[k], 0.0)
                row_l = row_l - (cm * l0 + ck * l1)
                row_r = row_r - (cm * r0 + ck * r1)
            s0 = lax.rsqrt(a)
            s1 = lax.rsqrt(det) * (a * s0)
            ratio = b * s0 * s0
            out_l = jnp.where(sub == m, lm * s0, jnp.where(sub == k, (lk - ratio * lm) * s1, out_l))
            out_r = jnp.where(sub == m, rm * s0, jnp.where(sub == k, (rk - ratio * rm) * s1, out_r))
            for q in range(p + 1, groups):
                left[q] = left[q] - (column[q][m] * l0 + column[q][k] * l1)
                right[q] = right[q] - (column[q][m] * r0 + column[q][k] * r1)
        upper.append(jnp.where(lane >= sub + 8 * p, out_l, 0.0))
        inverse.append(out_r)
    return jnp.concatenate(upper, 0), jnp.concatenate(inverse, 0)


def factor_kernel(packed_ref, barrier_ref, slab_ref, col_ref, diag_ref, panel_ref, work, upper):
    eye = lax.broadcasted_iota(jnp.int32, (128, 128), 0) == lax.broadcasted_iota(jnp.int32, (128, 128), 1)
    for k, (r, j) in enumerate(BLOCKS):
        block = packed_ref[16 * k : 16 * k + 16].reshape(128, 128)
        if r == j:
            block = block + jnp.where(eye, barrier_ref[:, 128 * r : 128 * r + 128], 0.0)
        work[128 * r : 128 * r + 128, 128 * j : 128 * j + 128] = block
    upper[...] = jnp.zeros(upper.shape, F32)
    rows = slab_ref[...]
    solved = []
    for b in range(NB):
        o = 128 * b
        u, inv = factor_block(work[o : o + 128, o : o + 128])
        upper[o : o + 128, o : o + 128] = u
        done = dot(rows[:, :128], inv, 1, 1, HIGHEST)
        solved.append(done)
        if b < NB - 1:
            beside = dot(inv, work[o : o + 128, o + 128 :], 1, 0, HIGHEST)
            upper[o : o + 128, o + 128 :] = beside
            for j in range(b + 1, NB):
                lead = beside[:, 128 * (j - b - 1) : 128 * (j - b)]
                tail = beside[:, 128 * (j - b - 1) :]
                work[128 * j : 128 * j + 128, 128 * j :] -= dot(lead, tail, 0, 0, HIGHEST)
            rows = rows[:, 128:] - dot(done, beside, 1, 0, HIGHEST)
    n_out = diag_ref.shape[0]
    first = col_ref[0] * n_out
    pick = lax.broadcasted_iota(jnp.int32, (n_out, DIAG), 1) == first + lax.broadcasted_iota(
        jnp.int32, (n_out, DIAG), 0
    )
    diag_ref[...] = dot(jnp.where(pick, 1.0, 0.0), upper[...], 1, 1, HIGHEST)
    panel_ref[...] = jnp.concatenate(solved, axis=1)[: panel_ref.shape[0]]


def factor(packed, barrier_diag, slab, col, diag_rows, panel_rows):
    vmem = pl.BlockSpec(memory_space=pltpu.VMEM)
    return pl.pallas_call(
        factor_kernel,
        name="factor",
        out_shape=(
            jax.ShapeDtypeStruct((diag_rows, DIAG), F32),
            jax.ShapeDtypeStruct((panel_rows, DIAG), F32),
        ),
        in_specs=[vmem] * 3 + [pl.BlockSpec(memory_space=pltpu.SMEM)],
        out_specs=[vmem] * 2,
        scratch_shapes=[pltpu.VMEM((DIAG, DIAG), F32), pltpu.VMEM((DIAG, DIAG), F32)],
    )(packed, barrier_diag.reshape(1, DIAG), slab, col)


def shards(
    inverse_factor, true_orders, slab_border, slab_columns, panel_border, panel_rows, barrier_diag
):
    n_scen, n_col = lax.axis_size("scen"), lax.axis_size("col")
    n_y = {16: 4, 4: 2}[n_col]
    packed, slab = exchange(
        n_col // n_y,
        n_y,
        n_scen // 2,
        true_orders,
        inverse_factor,
        slab_border,
        slab_columns,
        panel_border,
        panel_rows.reshape(1, -1),
    )
    col = lax.axis_index("col").astype(jnp.int32).reshape(1)
    return factor(packed, barrier_diag, slab, col, DIAG // n_col, 15)


def solution(mesh):
    in_specs = (
        P(("scen", "col"), None, None),
        P(("scen", "col")),
        P(("scen", "col"), None, None),
        P("scen", None),
        P("col", "scen", None, None),
        P("col", "scen", None),
        P(),
    )
    out_specs = (P("col", None), P(("scen", "col"), None))
    return jax.shard_map(shards, mesh=mesh, in_specs=in_specs, out_specs=out_specs, check_vma=False)
```

time: 740 us -> 110 us (0.15)
  waiting for transfers between devices: 489 us -> 0 us
  other arithmetic: 127 us -> 0 us
  Pallas kernels: 0 us -> 108 us
  matrix products: 51 us -> 0 us
  local copies, waits for them, and re-layouts: 49.6 us -> 0.69 us
  between operations: 19.7 us -> 1.31 us
    psum x1 -> x0, waiting for transfers between devices: 312 us -> none  [shards(): lax.psum(diag_partial, ('scen', 'col')) + jnp.diag(barrier_diag)]
    unnamed x4 -> x0, waiting for transfers between devices: 177 us -> none
    another operation x18 -> x0, other arithmetic: 124 us -> none  [the longest x14 82.8 us: shards(): factor_full = jnp.linalg.cholesky(schur_diag)]
    pallas_call x0 -> x2, Pallas kernels: none -> 108 us  [the longest x1 85.6 us: exchange(): pl.pallas_call(functools.partial(exchange_kernel, n_x, n_y, n_zy), name='...]
    dot_general x52 -> x0, matrix products: 42.8 us -> none  [the longest x16 18.7 us: panel_step(): jnp.einsum('bp,jp->bj', border_values, moved_rows, preferred_element_type...]
    another operation x34 -> x0, local copies, waits for them, and re-layouts: 15.3 us -> none
    dynamic_slice x18 -> x0, local copies, waits for them, and re-layouts: 12.1 us -> none  [the longest x16 11.2 us: shards(): lax.scan(panel_step, zero_panel, (group_border, lax.all_gather(transforme...]
    eq x16 -> x0, local copies, waits for them, and re-layouts: 11.2 us -> none  [spread_map(): index[:, None] == jnp.arange(width, dtype=jnp.int32)[None, :]]
  transfers between devices with their start and end apart: 3 -> 0, of which waited for: 2 -> 0; matrix products, arithmetic and copies ran while one was open for 20% -> 0% of each run, Pallas kernels for 0% -> 0%
where the time goes in v1:
time: 110 us
  Pallas kernels  108 us (98%)
  between operations  1.31 us (1%)
    pallas_call x1, Pallas kernels, exchange(): pl.pallas_call(functools.partial(exchange_kernel, n_x, n_y, n_zy), name='...  85.6 us
    pallas_call x1, Pallas kernels, factor(): pl.pallas_call(factor_kernel, name='factor', out_shape=(jax.ShapeDtypeStr...  22.3 us

profile of v1, /device:TPU:1, one launch (start us, length us, event | category | flops | bytes accessed | tf_op | source)
XLA Modules:
  0.0 109.9 jit_solution(17460649770366361257)
XLA Ops:
  0.6 0.0 copy-start
  1.3 0.0 copy-done
  1.3 0.7 reshape.13.rows_ref
  2.0 85.6 %exchange.1 = (f32[160,8,128]{2,1,0:T(8,128)}, f32[16,512]{1,0:T(8,128)}) custom-call(s32[1]{0:T(128)S(6)} %copy.9.order_ref, bf16[1,512,512]{2,1,0:T(8,128)(2,1)} %inv_ref.1, bf16[1,256,512]{2,1,0:T(8,128)(2,1)} %border_ref.1, s32[16,256]{1,0:T(8,128)} %columns_ref.1, bf16[1,16,48,512]{3,2,1,0:T(8,128)(2,1)} %panel_ref.1, s32[1,768]{1,0:T(1,128)} %reshape.13.rows_ref), custom_call_target="tpu_custom_call" | custom-call | tf_op jit(solution)/shard_map/exchange/pallas_call | solution.py:225
  87.6 22.3 %factor.1 = (f32[32,512]{1,0:T(8,128)}, f32[15,512]{1,0:T(8,128)}) custom-call(f32[160,8,128]{2,1,0:T(8,128)} %get-tuple-element.4.packed_ref, f32[1,512]{1,0:T(1,128)} %bitcast.2, f32[16,512]{1,0:T(8,128)} %get-tuple-element.5.slab_ref, s32[1]{0:T(128)} %bitcast.1.col_ref), custom_call_target="tpu_custom_call" | custom-call | tf_op jit(solution)/shard_map/factor/pallas_call | solution.py:351
Async XLA Ops:
  0.6 0.7 copy-start

commit v2 on v0

v2 whole, which is shorter than its diff:
```python
import functools

import jax
import jax.numpy as jnp
from jax import lax
from jax.experimental import pallas as pl
from jax.experimental.pallas import tpu as pltpu
from jax.sharding import PartitionSpec as P

HIGHEST = lax.Precision.HIGHEST
MESH = pl.DeviceIdType.MESH
F32 = jnp.float32
BF16 = jnp.bfloat16
DIAG = 512
NB = DIAG // 128
BLOCKS = [(r, j) for r in range(NB) for j in range(r, NB)]
TILES = 16 * len(BLOCKS)


def split(value, parts):
    out = []
    for _ in range(parts - 1):
        piece = value.astype(BF16)
        out.append(piece)
        value = value - piece.astype(F32)
    return out + [value.astype(BF16)]


def dot(a, b, ca, cb, precision=None):
    return lax.dot_general(
        a, b, (((ca,), (cb,)), ((), ())), precision=precision, preferred_element_type=F32
    )


def one_hot(targets, height):
    width = targets.shape[1]
    place = lax.broadcasted_iota(jnp.int32, (height, width), 0)
    return jnp.where(place == targets, 1.0, 0.0).astype(BF16)


class Wire:
    def __init__(self, send_sem, recv_sem):
        self.send_sem, self.recv_sem, self.used, self.sends = send_sem, recv_sem, 0, []

    def start(self, src, dst, scen, col):
        k = self.used
        self.used += 1
        copy = pltpu.make_async_remote_copy(
            src_ref=src,
            dst_ref=dst,
            send_sem=self.send_sem.at[k],
            recv_sem=self.recv_sem.at[k],
            device_id=(scen, col),
            device_id_type=MESH,
        )
        copy.start()
        self.sends.append(copy)
        return copy

    def drain(self):
        for copy in self.sends:
            copy.wait_send()


def factor_block(block):
    groups = 16
    tile = (8, 128)
    lane = lax.broadcasted_iota(jnp.int32, tile, 1)
    sub = lax.broadcasted_iota(jnp.int32, tile, 0)
    whole = (groups,) + tile
    left = block.reshape(whole)
    place = 8 * lax.broadcasted_iota(jnp.int32, whole, 0) + lax.broadcasted_iota(jnp.int32, whole, 1)
    right = jnp.where(lax.broadcasted_iota(jnp.int32, whole, 2) == place, 1.0, 0.0)
    upper, inverse = [], []

    def spread(row):
        return jnp.broadcast_to(row, tile)

    for p in range(groups):
        shape = (groups - p,) + tile
        column = [jnp.broadcast_to(left[:, :, 8 * p + m : 8 * p + m + 1], shape) for m in range(8)]
        row_l, row_r = left[0], right[0]
        left, right = left[1:], right[1:]
        out_l, out_r = jnp.zeros(tile, F32), jnp.zeros(tile, F32)
        for t in range(4):
            m, k = 2 * t, 2 * t + 1
            col_m, col_k = column[m], column[k]
            a, b, c = spread(col_m[0, m : m + 1]), spread(col_k[0, m : m + 1]), spread(col_k[0, k : k + 1])
            det = a * c - b * b
            over = 1.0 / det
            ia, ib, ic = c * over, -(b * over), a * over
            for n in range(k + 1, 8):
                e, f = spread(column[n][0, m : m + 1]), spread(column[n][0, k : k + 1])
                g, h = ia * e + ib * f, ib * e + ic * f
                column[n] = column[n] - (col_m * g + col_k * h)
            lm, lk = spread(row_l[m : m + 1]), spread(row_l[k : k + 1])
            rm, rk = spread(row_r[m : m + 1]), spread(row_r[k : k + 1])
            l0, l1 = ia * lm + ib * lk, ib * lm + ic * lk
            r0, r1 = ia * rm + ib * rk, ib * rm + ic * rk
            if k < 7:
                cm = jnp.where(sub > k, col_m[0], 0.0)
                ck = jnp.where(sub > k, col_k[0], 0.0)
                row_l = row_l - (cm * l0 + ck * l1)
                row_r = row_r - (cm * r0 + ck * r1)
            s0 = lax.rsqrt(a)
            s1 = lax.rsqrt(det) * (a * s0)
            ratio = b * s0 * s0
            out_l = jnp.where(sub == m, lm * s0, jnp.where(sub == k, (lk - ratio * lm) * s1, out_l))
            out_r = jnp.where(sub == m, rm * s0, jnp.where(sub == k, (rk - ratio * rm) * s1, out_r))
            if p < groups - 1:
                left = left - (col_m[1:] * l0 + col_k[1:] * l1)
                right = right - (col_m[1:] * r0 + col_k[1:] * r1)
        upper.append(jnp.where(lane >= sub + 8 * p, out_l, 0.0))
        inverse.append(out_r)
    return jnp.concatenate(upper, 0), jnp.concatenate(inverse, 0)


def kernel(
    n_x, n_y, n_z,
    order_ref, columns_ref, rows_ref, bar_ref, inv_ref, border_ref, panel_ref,
    diag_ref, slab_ref,
    factor_in, border_in, pb, tr, coup, coup_in, packed, c_buf, half, z_buf, z_sum, l_buf, y_own, y_buf,
    x_own, x_buf, full, maps, flat_buf, row_map, wide, total, pc_buf, p_half, pz_buf,
    work, upper, inverse,
    send_sem, recv_sem, local_sem,
):
    scen, col = lax.axis_index("scen"), lax.axis_index("col")
    core, l, z = scen % 2, (scen // 2) % 2, scen // 4
    x, y = col // n_y, col % n_y
    zy, n_zy = scen // 2, 2 * n_z
    sibling = scen + 1 - 2 * core
    beside_y = scen + 2 - 4 * l
    n_tiles = TILES // 2
    z_chunk = n_tiles // n_z
    chunk = z_chunk // 2
    p_rows = total.shape[0] // 2
    p_chunk = p_rows // n_zy
    p_size = inv_ref.shape[1]
    wire = Wire(send_sem, recv_sem)

    with jax.named_scope("barrier"):
        loads = [
            pltpu.make_async_copy(inv_ref.at[0], factor_in, local_sem.at[0]),
            pltpu.make_async_copy(border_ref.at[0], border_in, local_sem.at[1]),
            pltpu.make_async_copy(panel_ref.at[0, pl.ds(x * n_y, n_y)], pb.at[:, x], local_sem.at[2]),
        ]
        for load in loads:
            load.start()
        barrier = pltpu.get_barrier_semaphore()
        zy_peers = [((zy + d) % n_zy) * 2 + core for d in range(1, n_zy)]
        z_peers = [(z + d) % n_z for d in range(1, n_z)]
        y_peers = [(y + d) % n_y for d in range(1, n_y)]
        x_peers = [(x + d) % n_x for d in range(1, n_x)]
        greet = [(sibling, col)] + [(p, col) for p in zy_peers]
        greet += [(scen, x * n_y + p) for p in y_peers] + [(scen, p * n_y + y) for p in x_peers]
        for device in greet:
            pl.semaphore_signal(barrier, inc=1, device_id=device, device_id_type=MESH)
        pl.semaphore_wait(barrier, len(greet))

    def z_device(p):
        return p * 4 + l * 2 + core

    with jax.named_scope("transform"):
        pb_copies = [
            wire.start(panel_ref.at[0, pl.ds(p * n_y, n_y)], pb.at[:, x], scen, p * n_y + y) for p in x_peers
        ]
        loads[0].wait()
        loads[1].wait()
        order = order_ref[0]
        border = border_in[...]
        inside = lax.broadcasted_iota(jnp.int32, border.shape, 1) < order
        cut = jnp.where(inside, border.astype(F32), 0.0).astype(BF16)
        moved = dot(cut, factor_in[...], 1, 0)
        moved = jnp.where(inside, moved, 0.0).astype(BF16)
        tr[y] = moved
        near = [(y + 1) % n_y] + ([(y + n_y - 1) % n_y] if n_y > 2 else [])
        tr_copies = [wire.start(tr.at[y], tr.at[y], scen, x * n_y + p) for p in near]

    with jax.named_scope("diag"):
        terms = 0.5 * (dot(border, moved, 1, 1) + dot(moved, border, 1, 1))
        own_map = one_hot(columns_ref[pl.ds(col, 1), :], DIAG)
        spread = sum(dot(own_map, piece, 1, 0) for piece in split(terms, 3))
        pieces = split(spread, 3)
        base = 0
        for r in range(NB):
            rows = slice(128 * r, 128 * r + 128)
            strip = sum(dot(piece[rows], own_map[128 * r :], 1, 1) for piece in pieces)
            for j in range(r, NB):
                block = strip[:, 128 * (j - r) : 128 * (j - r + 1)]
                packed[base : base + 16] = block.reshape(16, 8, 128)
                base += 16

    with jax.named_scope("cores"):
        c_copy = wire.start(packed.at[pl.ds((1 - core) * n_tiles, n_tiles)], c_buf, sibling, col)
        n_scen, n_b = rows_ref.shape[1:]
        for i in range(n_scen):
            flat_buf[:, n_b * i : n_b * i + n_b] = rows_ref[0, i : i + 1, :]
        flat = flat_buf[...]
        owner = (flat * 4370) >> 16
        slot = (owner % 2) * p_rows + (owner // 2) * p_chunk + (flat - owner * 15)
        row_map[...] = one_hot(slot, 2 * p_rows)
        c_copy.wait_recv()
        half[...] = packed[pl.ds(core * n_tiles, n_tiles)] + c_buf[...]

    with jax.named_scope("z_sum"):
        z_copies = [
            wire.start(half.at[pl.ds(p * z_chunk, z_chunk)], z_buf.at[k], z_device(p), col)
            for k, p in enumerate(z_peers)
        ]

        def build_map(i, carry):
            maps[i] = one_hot(columns_ref[pl.ds(i, 1), :], DIAG)
            return carry

        lax.fori_loop(0, n_scen, build_map, 0)
    with jax.named_scope("z_wait"):
        for copy in z_copies:
            copy.wait_recv()
        z_sum[...] = half[pl.ds(z * z_chunk, z_chunk)]
        if n_z > 1:
            z_sum[...] += jnp.sum(z_buf[...], axis=0)
    with jax.named_scope("l_wait"):
        l_copy = wire.start(z_sum.at[pl.ds((1 - l) * chunk, chunk)], l_buf, beside_y, col)
        l_copy.wait_recv()
        y_own[...] = z_sum[pl.ds(l * chunk, chunk)] + l_buf[...]
        y_copies = [wire.start(y_own, y_buf.at[k], scen, x * n_y + p) for k, p in enumerate(y_peers)]

    with jax.named_scope("tr_wait"):
        for copy in tr_copies:
            copy.wait_recv()
        far_copies = []
        if n_y == 4:
            h = tr.shape[1] // 2
            up, down = (y + 1) % n_y, (y + n_y - 1) % n_y
            first, second = tr.at[down, pl.ds(0, h)], tr.at[up, pl.ds(h, h)]
            far_copies = [
                wire.start(first, first, scen, x * n_y + up),
                wire.start(second, second, scen, x * n_y + down),
            ]
        loads[2].wait()
        for copy in pb_copies:
            copy.wait_recv()

    def couple(i):
        stacked = pb[i].reshape(n_x * n_b, p_size)
        coup[i] = dot(stacked, tr[i], 1, 1).reshape(coup.shape[1:])
        coup_in[x * n_y + i] = coup[i, x]

    def give(i):
        return [wire.start(coup.at[i, p], coup_in.at[x * n_y + i], scen, p * n_y + y) for p in x_peers]

    with jax.named_scope("couple"):
        for i in [y] + near:
            couple(i)
    with jax.named_scope("y_wait"):
        for copy in y_copies:
            copy.wait_recv()
        x_own[...] = y_own[...] + jnp.sum(y_buf[...], axis=0)
        x_copies = [wire.start(x_own, x_buf.at[k], scen, p * n_y + y) for k, p in enumerate(x_peers)]
        q_copies = [copy for i in [y] + near for copy in give(i)]
    with jax.named_scope("x_wait"):
        for copy in x_copies:
            copy.wait_recv()
        mine = pl.ds(((core * n_z + z) * 2 + l) * chunk, chunk)
        full[mine] = x_own[...] + jnp.sum(x_buf[...], axis=0) if n_x > 1 else x_own[...]
    with jax.named_scope("l_gather"):
        lg_copy = wire.start(full.at[mine], full.at[mine], beside_y, col)
        lg_copy.wait_recv()
    with jax.named_scope("z_gather"):
        pair = pl.ds((core * n_z + z) * z_chunk, z_chunk)
        zg_copies = [wire.start(full.at[pair], full.at[pair], z_device(p), col) for p in z_peers]
        for copy in far_copies:
            copy.wait_recv()
        if n_y == 4:
            far = (y + 2) % n_y
            couple(far)
            q_copies += give(far)
    with jax.named_scope("q_wait"):
        for copy in q_copies:
            copy.wait_recv()

    with jax.named_scope("widen"):

        def widen(i, carry):
            high, low = split(coup_in[i], 2)
            both = dot(jnp.concatenate([high, low], axis=0), maps[i], 1, 1)
            wide[pl.ds(i * n_b, n_b), :] = both[:n_b] + both[n_b:]
            return carry

        lax.fori_loop(0, n_scen, widen, 0)
        high, low = split(wide[...], 2)
        total[...] = dot(row_map[...], high, 1, 0) + dot(row_map[...], low, 1, 0)
        pc_copy = wire.start(total.at[pl.ds((1 - core) * p_rows, p_rows)], pc_buf, sibling, col)

    with jax.named_scope("zg_wait"):
        for copy in zg_copies:
            copy.wait_recv()
        side = pl.ds(core * n_tiles, n_tiles)
        h_copy = wire.start(full.at[side], full.at[side], sibling, col)
    with jax.named_scope("pc_wait"):
        pc_copy.wait_recv()
        p_half[...] = total[pl.ds(core * p_rows, p_rows)] + pc_buf[...]
        pz_copies = [
            wire.start(p_half.at[pl.ds(((zy + d) % n_zy) * p_chunk, p_chunk)], pz_buf.at[d - 1], zy_peers[d - 1], col)
            for d in range(1, n_zy)
        ]
        upper[...] = jnp.zeros(upper.shape, F32)
    with jax.named_scope("h_wait"):
        h_copy.wait_recv()

    with jax.named_scope("load"):
        rr = lax.broadcasted_iota(jnp.int32, (128, 128), 0)
        cc = lax.broadcasted_iota(jnp.int32, (128, 128), 1)
        for k, (r, j) in enumerate(BLOCKS):
            block = full[16 * k : 16 * k + 16].reshape(128, 128)
            if r == j:
                block = block + jnp.where(rr == cc, bar_ref[:, 128 * r : 128 * r + 128], 0.0)
            work[128 * r : 128 * r + 128, 128 * j : 128 * j + 128] = block

    def step(b, carry):
        o = pl.multiple_of(b * 128, 128)
        with jax.named_scope("block"):
            u, inv = factor_block(work[pl.ds(o, 128), pl.ds(o, 128)])
            upper[pl.ds(o, 128), pl.ds(o, 128)] = u
            inverse[pl.ds(o, 128), :] = inv
        for k in range(NB - 1):

            @pl.when(b == k)
            def _():
                with jax.named_scope("trail"):
                    s = 128 * k
                    beside = dot(inv, work[s : s + 128, s + 128 :], 1, 0, HIGHEST)
                    upper[s : s + 128, s + 128 :] = beside
                    for j in range(k + 1, NB):
                        lead = beside[:, 128 * (j - k - 1) : 128 * (j - k)]
                        tail = beside[:, 128 * (j - k - 1) :]
                        work[128 * j : 128 * j + 128, 128 * j :] -= dot(lead, tail, 0, 0, HIGHEST)

        return carry

    lax.fori_loop(0, NB, step, 0)

    with jax.named_scope("pick"):
        n_out = diag_ref.shape[0]
        pick = lax.broadcasted_iota(jnp.int32, (n_out, DIAG), 1) == col * n_out + lax.broadcasted_iota(
            jnp.int32, (n_out, DIAG), 0
        )
        diag_ref[...] = dot(jnp.where(pick, 1.0, 0.0), upper[...], 1, 1, HIGHEST)
    with jax.named_scope("pz_wait"):
        for copy in pz_copies:
            copy.wait_recv()
    with jax.named_scope("solve"):
        rows = p_half[pl.ds(zy * p_chunk, p_chunk)] + jnp.sum(pz_buf[...], axis=0)
        solved = []
        for b in range(NB):
            done = dot(rows[:, :128], inverse[128 * b : 128 * b + 128, :], 1, 1, HIGHEST)
            solved.append(done)
            if b < NB - 1:
                rows = rows[:, 128:] - dot(done, upper[128 * b : 128 * b + 128, 128 * b + 128 :], 1, 0, HIGHEST)
        slab_ref[...] = jnp.concatenate(solved, axis=1)[: slab_ref.shape[0]]
    wire.drain()


def shards(
    inverse_factor, true_orders, slab_border, slab_columns, panel_border, panel_rows, barrier_diag
):
    n_col = lax.axis_size("col")
    n_z = lax.axis_size("scen") // 4
    n_y = min(n_col, 4) if n_col != 4 else 2
    n_x = n_col // n_y
    n_scen = slab_columns.shape[0]
    cbj, p_size = slab_border.shape[1:]
    cbp = panel_border.shape[2]
    z_chunk = TILES // 2 // n_z
    p_rows = 32 * n_z
    n_copies = 64
    tile = (8, 128)
    vmem = pl.BlockSpec(memory_space=pltpu.VMEM)
    anywhere = pl.BlockSpec(memory_space=pl.ANY)
    scratch = [
        ((p_size, p_size), BF16),
        ((cbj, p_size), BF16),
        ((n_y, n_x, cbp, p_size), BF16),
        ((n_y, cbj, p_size), BF16),
        ((n_y, n_x, cbp, cbj), F32),
        ((n_scen, cbp, cbj), F32),
        ((TILES,) + tile, F32),
        ((TILES // 2,) + tile, F32),
        ((TILES // 2,) + tile, F32),
        ((max(n_z - 1, 1), z_chunk) + tile, F32),
        ((z_chunk,) + tile, F32),
        ((z_chunk // 2,) + tile, F32),
        ((z_chunk // 2,) + tile, F32),
        ((n_y - 1, z_chunk // 2) + tile, F32),
        ((z_chunk // 2,) + tile, F32),
        ((max(n_x - 1, 1), z_chunk // 2) + tile, F32),
        ((TILES,) + tile, F32),
        ((n_scen, DIAG, cbj), BF16),
        ((1, n_scen * cbp), jnp.int32),
        ((2 * p_rows, n_scen * cbp), BF16),
        ((n_scen * cbp, DIAG), F32),
        ((2 * p_rows, DIAG), F32),
        ((p_rows, DIAG), F32),
        ((p_rows, DIAG), F32),
        ((2 * n_z - 1, 16, DIAG), F32),
        ((DIAG, DIAG), F32),
        ((DIAG, DIAG), F32),
        ((DIAG, 128), F32),
    ]
    return pl.pallas_call(
        functools.partial(kernel, n_x, n_y, n_z),
        name="slab",
        out_shape=(
            jax.ShapeDtypeStruct((DIAG // n_col, DIAG), F32),
            jax.ShapeDtypeStruct((15, DIAG), F32),
        ),
        in_specs=[pl.BlockSpec(memory_space=pltpu.SMEM)] + [vmem] * 3 + [anywhere] * 3,
        out_specs=[vmem] * 2,
        scratch_shapes=[pltpu.VMEM(*one) for one in scratch]
        + [
            pltpu.SemaphoreType.DMA((n_copies,)),
            pltpu.SemaphoreType.DMA((n_copies,)),
            pltpu.SemaphoreType.DMA((3,)),
        ],
        compiler_params=pltpu.CompilerParams(collective_id=0, has_side_effects=True),
    )(
        true_orders,
        slab_columns,
        panel_rows,
        barrier_diag.reshape(1, DIAG),
        inverse_factor,
        slab_border,
        panel_border,
    )


def solution(mesh):
    in_specs = (
        P(("scen", "col"), None, None),
        P(("scen", "col")),
        P(("scen", "col"), None, None),
        P("scen", None),
        P("col", "scen", None, None),
        P("col", "scen", None),
        P(),
    )
    out_specs = (P("col", None), P(("scen", "col"), None))
    return jax.shard_map(shards, mesh=mesh, in_specs=in_specs, out_specs=out_specs, check_vma=False)
```

time: 740 us -> 82.6 us (0.11)
  waiting for transfers between devices: 489 us -> 0 us
  other arithmetic: 127 us -> 0 us
  Pallas kernels: 0 us -> 78.9 us
  matrix products: 51 us -> 0 us
  local copies, waits for them, and re-layouts: 49.6 us -> 2.1 us
  between operations: 19.7 us -> 1.29 us
    psum x1 -> x0, waiting for transfers between devices: 312 us -> none  [shards(): lax.psum(diag_partial, ('scen', 'col')) + jnp.diag(barrier_diag)]
    unnamed x4 -> x0, waiting for transfers between devices: 177 us -> none
    another operation x18 -> x0, other arithmetic: 124 us -> none  [the longest x14 82.8 us: shards(): factor_full = jnp.linalg.cholesky(schur_diag)]
    pallas_call x0 -> x1, Pallas kernels: none -> 78.9 us  [shards(): pl.pallas_call(functools.partial(kernel, n_x, n_y, n_z), name='slab', out...]
    dot_general x52 -> x0, matrix products: 42.8 us -> none  [the longest x16 18.7 us: panel_step(): jnp.einsum('bp,jp->bj', border_values, moved_rows, preferred_element_type...]
    another operation x34 -> x0, local copies, waits for them, and re-layouts: 15.3 us -> none
    dynamic_slice x18 -> x0, local copies, waits for them, and re-layouts: 12.1 us -> none  [the longest x16 11.2 us: shards(): lax.scan(panel_step, zero_panel, (group_border, lax.all_gather(transforme...]
    eq x16 -> x0, local copies, waits for them, and re-layouts: 11.2 us -> none  [spread_map(): index[:, None] == jnp.arange(width, dtype=jnp.int32)[None, :]]
  transfers between devices with their start and end apart: 3 -> 0, of which waited for: 2 -> 0; matrix products, arithmetic and copies ran while one was open for 20% -> 0% of each run, Pallas kernels for 0% -> 0%
where the time goes in v2:
time: 82.6 us; the launch traced here: 82.3 us
  Pallas kernels  78.9 us (96%)
  local copies, waits for them, and re-layouts  2.1 us (3%)
  between operations  1.29 us (2%)
    pallas_call x1, Pallas kernels, shards(): pl.pallas_call(functools.partial(kernel, n_x, n_y, n_z), name='slab', out...  78.9 us
    unnamed x4, local copies, waits for them, and re-layouts  2.1 us

profile of v2, /device:TPU:1, one launch (start us, length us, event | category | flops | bytes accessed | tf_op | source)
XLA Modules:
  0.0 82.3 jit_solution(10986406398248792623)
XLA Ops:
  1.3 78.9 %slab.1 = (f32[32,512]{1,0:T(8,128)}, f32[15,512]{1,0:T(8,128)}) custom-call(s32[1]{0:T(128)S(6)} %copy.11.order_ref, s32[16,256]{1,0:T(8,128)} %columns_ref.1, s32[1,16,48]{2,1,0:T(8,128)} %rows_ref.1, f32[1,512]{1,0:T(1,128)} %bitcast.1, bf16[1,512,512]{2,1,0:T(8,128)(2,1)} %inv_ref.1, bf16[1,256,512]{2,1,0:T(8,128)(2,1)} %border_ref.1, ...), custom_call_target="tpu_custom_call" | custom-call | tf_op jit(solution)/shard_map/slab/pallas_call | solution.py:410
  80.2 0.0 copy-start
  80.2 1.5 %copy.12 = f32[32,512]{1,0:T(8,128)} copy(f32[32,512]{1,0:T(8,128)} %get-tuple-element.4) | data formatting | bytes 131072
  81.7 0.0 copy-done
  81.7 0.6 copy.13
Async XLA Ops:
  80.2 1.5 %copy-start = (f32[15,512]{1,0:T(8,128)S(1)}, f32[15,512]{1,0:T(8,128)}, u32[]{:S(2)}) copy-start(f32[15,512]{1,0:T(8,128)} %get-tuple-element.5) | copy-start | bytes 92164

commit v3 on v2

v3 whole, which is shorter than its diff:
```python
import functools

import jax
import jax.numpy as jnp
from jax import lax
from jax.experimental import pallas as pl
from jax.experimental.pallas import tpu as pltpu
from jax.sharding import PartitionSpec as P

HIGHEST = lax.Precision.HIGHEST
MESH = pl.DeviceIdType.MESH
F32 = jnp.float32
BF16 = jnp.bfloat16
DIAG = 512
NB = DIAG // 128
BLOCKS = [(r, j) for r in range(NB) for j in range(r, NB)]
TILES = 16 * len(BLOCKS)


def split(value, parts):
    out = []
    for _ in range(parts - 1):
        piece = value.astype(BF16)
        out.append(piece)
        value = value - piece.astype(F32)
    return out + [value.astype(BF16)]


def dot(a, b, ca, cb, precision=None):
    return lax.dot_general(
        a, b, (((ca,), (cb,)), ((), ())), precision=precision, preferred_element_type=F32
    )


def one_hot(targets, height):
    width = targets.shape[1]
    place = lax.broadcasted_iota(jnp.int32, (height, width), 0)
    return jnp.where(place == targets, 1.0, 0.0).astype(BF16)


class Wire:
    def __init__(self, send_sem, recv_sem):
        self.send_sem, self.recv_sem, self.used, self.sends = send_sem, recv_sem, 0, []

    def start(self, src, dst, scen, col):
        k = self.used
        self.used += 1
        copy = pltpu.make_async_remote_copy(
            src_ref=src,
            dst_ref=dst,
            send_sem=self.send_sem.at[k],
            recv_sem=self.recv_sem.at[k],
            device_id=(scen, col),
            device_id_type=MESH,
        )
        copy.start()
        self.sends.append(copy)
        return copy

    def drain(self, keep=0):
        done = len(self.sends) - keep
        for copy in self.sends[:done]:
            copy.wait_send()
        self.sends = self.sends[done:]


def factor_block(block):
    groups = 16
    tile = (8, 128)
    lane = lax.broadcasted_iota(jnp.int32, tile, 1)
    sub = lax.broadcasted_iota(jnp.int32, tile, 0)
    whole = (groups,) + tile
    left = block.reshape(whole)
    place = 8 * lax.broadcasted_iota(jnp.int32, whole, 0) + lax.broadcasted_iota(jnp.int32, whole, 1)
    right = jnp.where(lax.broadcasted_iota(jnp.int32, whole, 2) == place, 1.0, 0.0)
    upper, inverse = [], []

    def spread(row):
        return jnp.broadcast_to(row, tile)

    for p in range(groups):
        shape = (groups - p,) + tile
        column = [jnp.broadcast_to(left[:, :, 8 * p + m : 8 * p + m + 1], shape) for m in range(8)]
        row_l, row_r = left[0], right[0]
        left, right = left[1:], right[1:]
        out_l, out_r = jnp.zeros(tile, F32), jnp.zeros(tile, F32)
        for t in range(4):
            m, k = 2 * t, 2 * t + 1
            col_m, col_k = column[m], column[k]
            a, b, c = spread(col_m[0, m : m + 1]), spread(col_k[0, m : m + 1]), spread(col_k[0, k : k + 1])
            det = a * c - b * b
            over = 1.0 / det
            ia, ib, ic = c * over, -(b * over), a * over
            for n in range(k + 1, 8):
                e, f = spread(column[n][0, m : m + 1]), spread(column[n][0, k : k + 1])
                g, h = ia * e + ib * f, ib * e + ic * f
                column[n] = column[n] - (col_m * g + col_k * h)
            lm, lk = spread(row_l[m : m + 1]), spread(row_l[k : k + 1])
            rm, rk = spread(row_r[m : m + 1]), spread(row_r[k : k + 1])
            l0, l1 = ia * lm + ib * lk, ib * lm + ic * lk
            r0, r1 = ia * rm + ib * rk, ib * rm + ic * rk
            if k < 7:
                cm = jnp.where(sub > k, col_m[0], 0.0)
                ck = jnp.where(sub > k, col_k[0], 0.0)
                row_l = row_l - (cm * l0 + ck * l1)
                row_r = row_r - (cm * r0 + ck * r1)
            s0 = lax.rsqrt(a)
            s1 = lax.rsqrt(det) * (a * s0)
            ratio = b * s0 * s0
            out_l = jnp.where(sub == m, lm * s0, jnp.where(sub == k, (lk - ratio * lm) * s1, out_l))
            out_r = jnp.where(sub == m, rm * s0, jnp.where(sub == k, (rk - ratio * rm) * s1, out_r))
            if p < groups - 1:
                left = left - (col_m[1:] * l0 + col_k[1:] * l1)
                right = right - (col_m[1:] * r0 + col_k[1:] * r1)
        upper.append(jnp.where(lane >= sub + 8 * p, out_l, 0.0))
        inverse.append(out_r)
    return jnp.concatenate(upper, 0), jnp.concatenate(inverse, 0)


def kernel(
    n_x, n_y, n_z,
    order_ref, columns_ref, rows_ref, bar_ref, inv_ref, border_ref, panel_ref,
    diag_ref, slab_ref,
    order_in, columns_in, rows_in, bar_in, factor_in, border_in,
    pb, tr, coup, coup_in, packed, c_buf, half, z_buf, z_sum, l_buf, y_own, y_buf,
    x_own, x_buf, full, maps, flat_buf, row_map, wide, total, pc_buf, p_half, pz_buf,
    work, upper, inverse, turned,
    send_sem, recv_sem, local_sem,
):
    scen, col = lax.axis_index("scen"), lax.axis_index("col")
    core, l, z = scen % 2, (scen // 2) % 2, scen // 4
    x, y = col // n_y, col % n_y
    zy, n_zy = scen // 2, 2 * n_z
    sibling = scen + 1 - 2 * core
    beside_y = scen + 2 - 4 * l
    first, rest = 16 // n_z, 24 // n_z
    parts = (pl.ds(0, first), pl.ds(first, rest))
    p_rows = total.shape[0] // 2
    p_chunk = p_rows // n_zy
    p_size = inv_ref.shape[1]
    n_scen, n_b = rows_ref.shape[1:]
    wire = Wire(send_sem, recv_sem)

    with jax.named_scope("barrier"):
        loads = [
            pltpu.make_async_copy(src, dst, local_sem.at[k])
            for k, (src, dst) in enumerate(
                (
                    (inv_ref.at[0], factor_in),
                    (border_ref.at[0], border_in),
                    (order_ref, order_in),
                    (columns_ref, columns_in),
                    (rows_ref, rows_in),
                    (bar_ref, bar_in),
                    (panel_ref.at[0, pl.ds(x * n_y, n_y)], pb.at[:, x]),
                )
            )
        ]
        for load in loads:
            load.start()
        barrier = pltpu.get_barrier_semaphore()
        zy_peers = [((zy + d) % n_zy) * 2 + core for d in range(1, n_zy)]
        z_peers = [(z + d) % n_z for d in range(1, n_z)]
        y_peers = [(y + d) % n_y for d in range(1, n_y)]
        x_peers = [(x + d) % n_x for d in range(1, n_x)]
        greet = [(sibling, col)] + [(p, col) for p in zy_peers]
        greet += [(scen, x * n_y + p) for p in y_peers] + [(scen, p * n_y + y) for p in x_peers]
        for device in greet:
            pl.semaphore_signal(barrier, inc=1, device_id=device, device_id_type=MESH)

    def arrive(copies):
        for copy in copies:
            copy.wait_recv()

    with jax.named_scope("transform"):
        for load in loads[:4]:
            load.wait()
        order = order_in[0]
        border = border_in[...]
        inside = lax.broadcasted_iota(jnp.int32, border.shape, 1) < order
        cut = jnp.where(inside, border.astype(F32), 0.0).astype(BF16)
        moved = dot(cut, factor_in[...], 1, 0)
        moved = jnp.where(inside, moved, 0.0).astype(BF16)
        tr[y] = moved
        pl.semaphore_wait(barrier, len(greet))
        near = [(y + 1) % n_y] + ([(y + n_y - 1) % n_y] if n_y > 2 else [])
        tr_copies = [wire.start(tr.at[y], tr.at[y], scen, x * n_y + p) for p in near]
        pb_copies = [
            wire.start(panel_ref.at[0, pl.ds(p * n_y, n_y)], pb.at[:, x], scen, p * n_y + y) for p in x_peers
        ]

    with jax.named_scope("diag"):
        terms = 0.5 * (dot(border, moved, 1, 1) + dot(moved, border, 1, 1))
        own_map = one_hot(columns_in[pl.ds(col, 1), :], DIAG)
        spread = sum(dot(own_map, piece, 1, 0) for piece in split(terms, 3))
        pieces = split(spread, 3)
        c_copies = []
        for r in range(NB):
            rows = slice(128 * r, 128 * r + 128)
            strip = sum(dot(piece[rows], own_map[128 * r :], 1, 1) for piece in pieces)
            for j in range(r, NB):
                block = strip[:, 128 * (j - r) : 128 * (j - r + 1)]
                for t in range(16):
                    packed[where_tile(n_z, r, j, t)] = block[8 * t : 8 * t + 8]
            if r == 0:
                c_copies.append(
                    wire.start(packed.at[1 - core, :, :, parts[0]], c_buf.at[:, :, parts[0]], sibling, col)
                )
        c_copies.append(wire.start(packed.at[1 - core, :, :, parts[1]], c_buf.at[:, :, parts[1]], sibling, col))

    def add_cores(k):
        c_copies[k].wait_recv()
        half[:, :, parts[k]] = packed[core, :, :, parts[k]] + c_buf[:, :, parts[k]]
        return [
            wire.start(half.at[p, :, parts[k]], z_buf.at[i, :, parts[k]], p * 4 + l * 2 + core, col)
            for i, p in enumerate(z_peers)
        ]

    def add_z(k, copies):
        arrive(copies)
        mine = half[z, :, parts[k]]
        z_sum[:, parts[k]] = mine + jnp.sum(z_buf[:, :, parts[k]], axis=0) if n_z > 1 else mine
        return [wire.start(z_sum.at[1 - l, parts[k]], l_buf.at[parts[k]], beside_y, col)]

    def add_l(k, copies):
        arrive(copies)
        y_own[parts[k]] = z_sum[l, parts[k]] + l_buf[parts[k]]
        return [
            wire.start(y_own.at[parts[k]], y_buf.at[i, parts[k]], scen, x * n_y + p) for i, p in enumerate(y_peers)
        ]

    def add_y(k, copies):
        arrive(copies)
        x_own[parts[k]] = y_own[parts[k]] + jnp.sum(y_buf[:, parts[k]], axis=0)
        return [
            wire.start(x_own.at[parts[k]], x_buf.at[i, parts[k]], scen, p * n_y + y) for i, p in enumerate(x_peers)
        ]

    def add_x(k, copies):
        arrive(copies)
        full[core, z, l, parts[k]] = x_own[parts[k]] + jnp.sum(x_buf[:, parts[k]], axis=0)
        here = full.at[core, z, l, parts[k]]
        return [wire.start(here, here, beside_y, col)]

    def gather_z(k, copies):
        arrive(copies)
        here = full.at[core, z, :, parts[k]]
        return [wire.start(here, here, p * 4 + l * 2 + core, col) for p in z_peers]

    def gather_cores(k, copies):
        arrive(copies)
        here = full.at[core, :, :, parts[k]]
        return [wire.start(here, here, sibling, col)]

    def couple(i):
        stacked = pb[i].reshape(n_x * n_b, p_size)
        coup[i] = dot(stacked, tr[i], 1, 1).reshape(coup.shape[1:])
        coup_in[x * n_y + i] = coup[i, x]

    def give(i):
        return [wire.start(coup.at[i, p], coup_in.at[x * n_y + i], scen, p * n_y + y) for p in x_peers]

    def widen(i):
        high, low = split(coup_in[i], 2)
        both = dot(jnp.concatenate([high, low], axis=0), maps[i], 1, 1)
        at = i * n_b
        wide[pl.ds(pl.multiple_of(at, 16), n_b), :] = both[:n_b] + both[n_b:]

    with jax.named_scope("cores0"):
        s0 = add_cores(0)
    with jax.named_scope("cores1"):
        s1 = add_cores(1)
    with jax.named_scope("maps"):
        loads[4].wait()
        loads[5].wait()
        for i in range(n_scen):
            flat_buf[:, n_b * i : n_b * i + n_b] = rows_in[0, i : i + 1, :]
        flat = flat_buf[...]
        owner = (flat * 4370) >> 16
        slot = (owner % 2) * p_rows + (owner // 2) * p_chunk + (flat - owner * 15)
        row_map[...] = one_hot(slot, 2 * p_rows)

        def build_map(i, carry):
            maps[i] = one_hot(columns_in[pl.ds(i, 1), :], DIAG)
            return carry

        lax.fori_loop(0, n_scen, build_map, 0)
        upper[...] = jnp.zeros(upper.shape, F32)
    with jax.named_scope("z0"):
        s0 = add_z(0, s0)
    with jax.named_scope("l0"):
        s0 = add_l(0, s0)
    with jax.named_scope("z1"):
        s1 = add_z(1, s1)
    with jax.named_scope("tr_wait"):
        arrive(tr_copies)
        far_copies = []
        if n_y == 4:
            h = tr.shape[1] // 2
            up, down = (y + 1) % n_y, (y + n_y - 1) % n_y
            low_half, high_half = tr.at[down, pl.ds(0, h)], tr.at[up, pl.ds(h, h)]
            far_copies = [
                wire.start(low_half, low_half, scen, x * n_y + up),
                wire.start(high_half, high_half, scen, x * n_y + down),
            ]
        loads[6].wait()
        arrive(pb_copies)
    with jax.named_scope("couple"):
        for i in [y] + near:
            couple(i)
    with jax.named_scope("y0"):
        s0 = add_y(0, s0)
        q_near = [copy for i in [y] + near for copy in give(i)]
    with jax.named_scope("l1"):
        s1 = add_l(1, s1)
    with jax.named_scope("x0"):
        s0 = add_x(0, s0)
    with jax.named_scope("lg0"):
        s0 = gather_z(0, s0)
    with jax.named_scope("y1"):
        s1 = add_y(1, s1)
    with jax.named_scope("far"):
        q_far = []
        if n_y == 4:
            arrive(far_copies)
            far = (y + 2) % n_y
            couple(far)
            q_far = give(far)
    with jax.named_scope("q_near"):
        arrive(q_near)
    with jax.named_scope("widen_near"):
        for i in [y] + near:
            for k in range(n_x):
                widen(k * n_y + i)
    with jax.named_scope("x1"):
        s1 = add_x(1, s1)
    with jax.named_scope("zg0"):
        s0 = gather_cores(0, s0)
    with jax.named_scope("lg1"):
        s1 = gather_z(1, s1)
    with jax.named_scope("q_far"):
        arrive(q_far)
    with jax.named_scope("widen_far"):
        if n_y == 4:
            for k in range(n_x):
                widen(k * n_y + far)
    with jax.named_scope("total"):
        high, low = split(wide[...], 2)
        total[...] = dot(row_map[...], high, 1, 0) + dot(row_map[...], low, 1, 0)
        pc_copy = wire.start(total.at[pl.ds((1 - core) * p_rows, p_rows)], pc_buf, sibling, col)
    with jax.named_scope("drain0"):
        wire.drain(2 * n_z + 2)
    with jax.named_scope("hg0"):
        arrive(s0)

    rr = lax.broadcasted_iota(jnp.int32, (128, 128), 0)
    cc = lax.broadcasted_iota(jnp.int32, (128, 128), 1)

    def load_row(r):
        for j in range(r, NB):
            block = jnp.concatenate([full[where_tile(n_z, r, j, t)] for t in range(16)], axis=0)
            if r == j:
                block = block + jnp.where(rr == cc, bar_in[:, 128 * r : 128 * r + 128], 0.0)
            work[128 * r : 128 * r + 128, 128 * j : 128 * j + 128] = block

    def block_step(o):
        with jax.named_scope("block"):
            u, inv = factor_block(work[pl.ds(o, 128), pl.ds(o, 128)])
            upper[pl.ds(o, 128), pl.ds(o, 128)] = u
            inverse[pl.ds(o, 128), :] = inv
        return inv

    def trail(k, inv):
        with jax.named_scope("trail"):
            s = 128 * k
            beside = dot(inv, work[s : s + 128, s + 128 :], 1, 0, HIGHEST)
            upper[s : s + 128, s + 128 :] = beside
            for j in range(k + 1, NB):
                lead = beside[:, 128 * (j - k - 1) : 128 * (j - k)]
                tail = beside[:, 128 * (j - k - 1) :]
                work[128 * j : 128 * j + 128, 128 * j :] -= dot(lead, tail, 0, 0, HIGHEST)

    load_row(0)
    inv = block_step(0)
    with jax.named_scope("zg1"):
        s1 = gather_cores(1, s1)
    with jax.named_scope("hg1"):
        arrive(s1)
        for r in range(1, NB):
            load_row(r)
    trail(0, inv)
    with jax.named_scope("pc_wait"):
        pc_copy.wait_recv()
        p_half[...] = total[pl.ds(core * p_rows, p_rows)] + pc_buf[...]
        pz_copies = [
            wire.start(p_half.at[pl.ds(((zy + d) % n_zy) * p_chunk, p_chunk)], pz_buf.at[d - 1], zy_peers[d - 1], col)
            for d in range(1, n_zy)
        ]

    def step(b, carry):
        inv = block_step(pl.multiple_of(b * 128, 128))
        for k in range(1, NB - 1):

            @pl.when(b == k)
            def _():
                trail(k, inv)

        return carry

    lax.fori_loop(1, NB, step, 0)

    with jax.named_scope("pick"):
        n_out = diag_ref.shape[0]
        start = col * n_out
        turned[...] = jnp.transpose(upper[:, pl.ds(pl.multiple_of(start // 128 * 128, 128), 128)])
        diag_ref[...] = turned[pl.ds(pl.multiple_of(start % 128, 8), n_out), :]
    with jax.named_scope("pz_wait"):
        arrive(pz_copies)
    with jax.named_scope("solve"):
        rows = p_half[pl.ds(zy * p_chunk, p_chunk)] + jnp.sum(pz_buf[...], axis=0)
        solved = []
        for b in range(NB):
            done = dot(rows[:, :128], inverse[128 * b : 128 * b + 128, :], 1, 1, HIGHEST)
            solved.append(done)
            if b < NB - 1:
                rows = rows[:, 128:] - dot(done, upper[128 * b : 128 * b + 128, 128 * b + 128 :], 1, 0, HIGHEST)
        slab_ref[...] = jnp.concatenate(solved, axis=1)[: slab_ref.shape[0]]
    with jax.named_scope("drain1"):
        wire.drain()


def out_kernel(diag_ref, slab_ref, diag_out, slab_out):
    diag_out[...] = diag_ref[...]
    slab_out[...] = slab_ref[...]


def where_tile(n_z, r, j, t):
    first, rest = 16 // n_z, 24 // n_z
    at = 16 * BLOCKS.index((r, j)) + t
    if r == 0:
        chunk, e = at // first, at % first
    else:
        at -= 16 * NB
        chunk, e = at // rest, first + at % rest
    return chunk // (2 * n_z), chunk // 2 % n_z, chunk % 2, e


def shards(
    inverse_factor, true_orders, slab_border, slab_columns, panel_border, panel_rows, barrier_diag
):
    n_col = lax.axis_size("col")
    n_z = lax.axis_size("scen") // 4
    n_y = min(n_col, 4) if n_col != 4 else 2
    n_x = n_col // n_y
    n_scen = slab_columns.shape[0]
    cbj, p_size = slab_border.shape[1:]
    cbp = panel_border.shape[2]
    chunk = TILES // 4 // n_z
    p_rows = 32 * n_z
    n_copies = 96
    tile = (8, 128)
    vmem = pl.BlockSpec(memory_space=pltpu.VMEM)
    anywhere = pl.BlockSpec(memory_space=pl.ANY)
    scratch = [
        pltpu.SMEM((1,), jnp.int32),
        pltpu.VMEM(slab_columns.shape, jnp.int32),
        pltpu.VMEM(panel_rows.shape, jnp.int32),
        pltpu.VMEM((1, DIAG), F32),
        pltpu.VMEM((p_size, p_size), BF16),
        pltpu.VMEM((cbj, p_size), BF16),
        pltpu.VMEM((n_y, n_x, cbp, p_size), BF16),
        pltpu.VMEM((n_y, cbj, p_size), BF16),
        pltpu.VMEM((n_y, n_x, cbp, cbj), F32),
        pltpu.VMEM((n_scen, cbp, cbj), F32),
        pltpu.VMEM((2, n_z, 2, chunk) + tile, F32),
        pltpu.VMEM((n_z, 2, chunk) + tile, F32),
        pltpu.VMEM((n_z, 2, chunk) + tile, F32),
        pltpu.VMEM((max(n_z - 1, 1), 2, chunk) + tile, F32),
        pltpu.VMEM((2, chunk) + tile, F32),
        pltpu.VMEM((chunk,) + tile, F32),
        pltpu.VMEM((chunk,) + tile, F32),
        pltpu.VMEM((n_y - 1, chunk) + tile, F32),
        pltpu.VMEM((chunk,) + tile, F32),
        pltpu.VMEM((max(n_x - 1, 1), chunk) + tile, F32),
        pltpu.VMEM((2, n_z, 2, chunk) + tile, F32),
        pltpu.VMEM((n_scen, DIAG, cbj), BF16),
        pltpu.VMEM((1, n_scen * cbp), jnp.int32),
        pltpu.VMEM((2 * p_rows, n_scen * cbp), BF16),
        pltpu.VMEM((n_scen * cbp, DIAG), F32),
        pltpu.VMEM((2 * p_rows, DIAG), F32),
        pltpu.VMEM((p_rows, DIAG), F32),
        pltpu.VMEM((p_rows, DIAG), F32),
        pltpu.VMEM((2 * n_z - 1, 16, DIAG), F32),
        pltpu.VMEM((DIAG, DIAG), F32),
        pltpu.VMEM((DIAG, DIAG), F32),
        pltpu.VMEM((DIAG, 128), F32),
        pltpu.VMEM((128, DIAG), F32),
        pltpu.SemaphoreType.DMA((n_copies,)),
        pltpu.SemaphoreType.DMA((n_copies,)),
        pltpu.SemaphoreType.DMA((7,)),
    ]
    factored = pl.pallas_call(
        functools.partial(kernel, n_x, n_y, n_z),
        name="slab",
        out_shape=tuple(
            pltpu.VMEM(shape, F32) for shape in ((DIAG // n_col, DIAG), (15, DIAG))
        ),
        in_specs=[anywhere] * 7,
        out_specs=[vmem] * 2,
        scratch_shapes=scratch,
        compiler_params=pltpu.CompilerParams(collective_id=0, has_side_effects=True),
    )(
        true_orders,
        slab_columns,
        panel_rows,
        barrier_diag.reshape(1, DIAG),
        inverse_factor,
        slab_border,
        panel_border,
    )
    return pl.pallas_call(
        out_kernel,
        name="out",
        out_shape=(
            jax.ShapeDtypeStruct((DIAG // n_col, DIAG), F32),
            jax.ShapeDtypeStruct((15, DIAG), F32),
        ),
        in_specs=[vmem] * 2,
        out_specs=[vmem] * 2,
    )(*(pltpu.with_memory_space_constraint(one, pltpu.VMEM) for one in factored))


def solution(mesh):
    in_specs = (
        P(("scen", "col"), None, None),
        P(("scen", "col")),
        P(("scen", "col"), None, None),
        P("scen", None),
        P("col", "scen", None, None),
        P("col", "scen", None),
        P(),
    )
    out_specs = (P("col", None), P(("scen", "col"), None))
    return jax.shard_map(shards, mesh=mesh, in_specs=in_specs, out_specs=out_specs, check_vma=False)
```

time: 82.6 us -> 74.9 us (0.907)
  Pallas kernels: 78.9 us -> 73.4 us
  local copies, waits for them, and re-layouts: 2.1 us -> 0 us
    pallas_call x1, Pallas kernels: 78.9 us -> 72.8 us  [shards(): pl.pallas_call(functools.partial(kernel, n_x, n_y, n_z), name='slab', out...]
    unnamed x4 -> x0, local copies, waits for them, and re-layouts: 2.1 us -> none
where the time goes in v3:
time: 74.9 us; the launch traced here: 74.7 us
  Pallas kernels  73.4 us (98%)
  between operations  1.28 us (2%)
    pallas_call x1, Pallas kernels, shards(): pl.pallas_call(functools.partial(kernel, n_x, n_y, n_z), name='slab', out...  72.8 us

profile of v3, /device:TPU:1, one launch (start us, length us, event | category | flops | bytes accessed | tf_op | source)
XLA Modules:
  0.0 74.7 jit_solution(2935407928110217297)
XLA Ops:
  1.3 72.8 %slab.1 = (f32[32,512]{1,0:T(8,128)S(1)}, f32[15,512]{1,0:T(8,128)S(1)}) custom-call(s32[1]{0:T(128)S(6)} %copy.9.order_ref, s32[16,256]{1,0:T(8,128)} %columns_ref.1, s32[1,16,48]{2,1,0:T(8,128)} %rows_ref.1, f32[1,512]{1,0:T(1,128)} %bitcast.1, bf16[1,512,512]{2,1,0:T(8,128)(2,1)} %inv_ref.1, bf16[1,256,512]{2,1,0:T(8,128)(2,1)} %border_ref.1, ...), custom_call_target="tpu_custom_call" | custom-call | tf_op jit(solution)/shard_map/slab/pallas_call | solution.py:502
  74.1 0.6 out.1

commit v4 on v3

--- a/solution.py
+++ b/solution.py
@@ -42,20 +42,17 @@
     def __init__(self, send_sem, recv_sem):
         self.send_sem, self.recv_sem, self.used, self.sends = send_sem, recv_sem, 0, []
 
-    def start(self, src, dst, scen, col):
-        k = self.used
+    def start(self, group, view=None):
+        sems = self.send_sem.at[self.used], self.recv_sem.at[self.used]
         self.used += 1
-        copy = pltpu.make_async_remote_copy(
-            src_ref=src,
-            dst_ref=dst,
-            send_sem=self.send_sem.at[k],
-            recv_sem=self.recv_sem.at[k],
-            device_id=(scen, col),
-            device_id_type=MESH,
-        )
-        copy.start()
-        self.sends.append(copy)
-        return copy
+        for src, dst, scen, col in group:
+            pltpu.make_async_remote_copy(src, dst, *sems, (scen, col), MESH).start()
+        if group:
+            view = group[0][1] if view is None else view
+            whole = pltpu.make_async_remote_copy(view, view, *sems, group[0][2:], MESH)
+            self.sends.append(whole)
+            return [whole]
+        return []
 
     def drain(self, keep=0):
         done = len(self.sends) - keep
@@ -64,7 +61,13 @@
         self.sends = self.sends[done:]
 
 
-def factor_block(block):
+def tree(terms):
+    while len(terms) > 1:
+        terms = [sum(terms[i : i + 2]) for i in range(0, len(terms), 2)]
+    return terms[0]
+
+
+def factor_block(block, zero):
     groups = 16
     tile = (8, 128)
     lane = lax.broadcasted_iota(jnp.int32, tile, 1)
@@ -75,45 +78,53 @@
     right = jnp.where(lax.broadcasted_iota(jnp.int32, whole, 2) == place, 1.0, 0.0)
     upper, inverse = [], []
 
-    def spread(row):
-        return jnp.broadcast_to(row, tile)
+    def spread(value, m):
+        return jnp.broadcast_to(value[m : m + 1], tile)
 
     for p in range(groups):
-        shape = (groups - p,) + tile
-        column = [jnp.broadcast_to(left[:, :, 8 * p + m : 8 * p + m + 1], shape) for m in range(8)]
-        row_l, row_r = left[0], right[0]
-        left, right = left[1:], right[1:]
-        out_l, out_r = jnp.zeros(tile, F32), jnp.zeros(tile, F32)
-        for t in range(4):
-            m, k = 2 * t, 2 * t + 1
+        rows = [left[0], right[0]]
+        column = [jnp.broadcast_to(rows[0][:, 8 * p + m : 8 * p + m + 1], tile) + zero for m in range(8)]
+        out = [jnp.zeros(tile, F32)] * 2
+        below, solved = {}, [[None] * 8, [None] * 8]
+        for m in range(0, 8, 2):
+            k = m + 1
             col_m, col_k = column[m], column[k]
-            a, b, c = spread(col_m[0, m : m + 1]), spread(col_k[0, m : m + 1]), spread(col_k[0, k : k + 1])
+            a, b, c = spread(col_m, m), spread(col_k, m), spread(col_k, k)
             det = a * c - b * b
             over = 1.0 / det
             ia, ib, ic = c * over, -(b * over), a * over
             for n in range(k + 1, 8):
-                e, f = spread(column[n][0, m : m + 1]), spread(column[n][0, k : k + 1])
+                e, f = spread(column[n], m), spread(column[n], k)
                 g, h = ia * e + ib * f, ib * e + ic * f
+                below[m, n], below[k, n] = g, h
                 column[n] = column[n] - (col_m * g + col_k * h)
-            lm, lk = spread(row_l[m : m + 1]), spread(row_l[k : k + 1])
-            rm, rk = spread(row_r[m : m + 1]), spread(row_r[k : k + 1])
-            l0, l1 = ia * lm + ib * lk, ib * lm + ic * lk
-            r0, r1 = ia * rm + ib * rk, ib * rm + ic * rk
-            if k < 7:
-                cm = jnp.where(sub > k, col_m[0], 0.0)
-                ck = jnp.where(sub > k, col_k[0], 0.0)
-                row_l = row_l - (cm * l0 + ck * l1)
-                row_r = row_r - (cm * r0 + ck * r1)
             s0 = lax.rsqrt(a)
             s1 = lax.rsqrt(det) * (a * s0)
             ratio = b * s0 * s0
-            out_l = jnp.where(sub == m, lm * s0, jnp.where(sub == k, (lk - ratio * lm) * s1, out_l))
-            out_r = jnp.where(sub == m, rm * s0, jnp.where(sub == k, (rk - ratio * rm) * s1, out_r))
-            if p < groups - 1:
-                left = left - (col_m[1:] * l0 + col_k[1:] * l1)
-                right = right - (col_m[1:] * r0 + col_k[1:] * r1)
-        upper.append(jnp.where(lane >= sub + 8 * p, out_l, 0.0))
-        inverse.append(out_r)
+            under = sub > k
+            for w in range(2):
+                first, second = spread(rows[w], m), spread(rows[w], k)
+                y0, y1 = ia * first + ib * second, ib * first + ic * second
+                solved[w][m], solved[w][k] = y0, y1
+                if k < 7:
+                    rows[w] = rows[w] - jnp.where(under, col_m * y0 + col_k * y1, 0.0)
+                out[w] = jnp.where(
+                    sub == m, first * s0, jnp.where(sub == k, (second - ratio * first) * s1, out[w])
+                )
+        upper.append(jnp.where(lane >= sub + 8 * p, out[0], 0.0))
+        inverse.append(out[1])
+        if p == groups - 1:
+            break
+        for w in range(2):
+            for m in range(5, -1, -1):
+                late = [below[m, n] * solved[w][n] for n in range(m // 2 * 2 + 2, 8)]
+                solved[w][m] = solved[w][m] - tree(late)
+        next_l, next_r = [], []
+        for q in range(1, groups - p):
+            raw = [jnp.broadcast_to(left[q][:, 8 * p + m : 8 * p + m + 1], tile) for m in range(8)]
+            next_l.append(left[q] - tree([raw[m] * solved[0][m] for m in range(8)]))
+            next_r.append(right[q] - tree([raw[m] * solved[1][m] for m in range(8)]))
+        left, right = next_l, next_r
     return jnp.concatenate(upper, 0), jnp.concatenate(inverse, 0)
 
 
@@ -184,10 +195,13 @@
         tr[y] = moved
         pl.semaphore_wait(barrier, len(greet))
         near = [(y + 1) % n_y] + ([(y + n_y - 1) % n_y] if n_y > 2 else [])
-        tr_copies = [wire.start(tr.at[y], tr.at[y], scen, x * n_y + p) for p in near]
-        pb_copies = [
-            wire.start(panel_ref.at[0, pl.ds(p * n_y, n_y)], pb.at[:, x], scen, p * n_y + y) for p in x_peers
-        ]
+        tr_copies = wire.start(
+            [(tr.at[y], tr.at[y], scen, x * n_y + p) for p in near], tr.at[pl.ds(0, len(near))]
+        )
+        pb_copies = wire.start(
+            [(panel_ref.at[0, pl.ds(p * n_y, n_y)], pb.at[:, x], scen, p * n_y + y) for p in x_peers],
+            pb.at[:, pl.ds(0, n_x - 1)],
+        )
 
     with jax.named_scope("diag"):
         terms = 0.5 * (dot(border, moved, 1, 1) + dot(moved, border, 1, 1))
@@ -195,6 +209,10 @@
         spread = sum(dot(own_map, piece, 1, 0) for piece in split(terms, 3))
         pieces = split(spread, 3)
         c_copies = []
+
+        def give_core(k):
+            return wire.start([(packed.at[1 - core, :, :, parts[k]], c_buf.at[:, :, parts[k]], sibling, col)])
+
         for r in range(NB):
             rows = slice(128 * r, 128 * r + 128)
             strip = sum(dot(piece[rows], own_map[128 * r :], 1, 1) for piece in pieces)
@@ -203,62 +221,71 @@
                 for t in range(16):
                     packed[where_tile(n_z, r, j, t)] = block[8 * t : 8 * t + 8]
             if r == 0:
-                c_copies.append(
-                    wire.start(packed.at[1 - core, :, :, parts[0]], c_buf.at[:, :, parts[0]], sibling, col)
-                )
-        c_copies.append(wire.start(packed.at[1 - core, :, :, parts[1]], c_buf.at[:, :, parts[1]], sibling, col))
+                c_copies.append(give_core(0))
+        c_copies.append(give_core(1))
 
     def add_cores(k):
-        c_copies[k].wait_recv()
+        arrive(c_copies[k])
         half[:, :, parts[k]] = packed[core, :, :, parts[k]] + c_buf[:, :, parts[k]]
-        return [
-            wire.start(half.at[p, :, parts[k]], z_buf.at[i, :, parts[k]], p * 4 + l * 2 + core, col)
-            for i, p in enumerate(z_peers)
-        ]
+        return wire.start(
+            [
+                (half.at[p, :, parts[k]], z_buf.at[i, :, parts[k]], p * 4 + l * 2 + core, col)
+                for i, p in enumerate(z_peers)
+            ],
+            z_buf.at[:, :, parts[k]],
+        )
 
     def add_z(k, copies):
         arrive(copies)
         mine = half[z, :, parts[k]]
         z_sum[:, parts[k]] = mine + jnp.sum(z_buf[:, :, parts[k]], axis=0) if n_z > 1 else mine
-        return [wire.start(z_sum.at[1 - l, parts[k]], l_buf.at[parts[k]], beside_y, col)]
+        return wire.start([(z_sum.at[1 - l, parts[k]], l_buf.at[parts[k]], beside_y, col)])
 
     def add_l(k, copies):
         arrive(copies)
         y_own[parts[k]] = z_sum[l, parts[k]] + l_buf[parts[k]]
-        return [
-            wire.start(y_own.at[parts[k]], y_buf.at[i, parts[k]], scen, x * n_y + p) for i, p in enumerate(y_peers)
-        ]
+        return wire.start(
+            [(y_own.at[parts[k]], y_buf.at[i, parts[k]], scen, x * n_y + p) for i, p in enumerate(y_peers)],
+            y_buf.at[:, parts[k]],
+        )
 
     def add_y(k, copies):
         arrive(copies)
         x_own[parts[k]] = y_own[parts[k]] + jnp.sum(y_buf[:, parts[k]], axis=0)
-        return [
-            wire.start(x_own.at[parts[k]], x_buf.at[i, parts[k]], scen, p * n_y + y) for i, p in enumerate(x_peers)
-        ]
+        return wire.start(
+            [(x_own.at[parts[k]], x_buf.at[i, parts[k]], scen, p * n_y + y) for i, p in enumerate(x_peers)],
+            x_buf.at[:, parts[k]],
+        )
 
     def add_x(k, copies):
         arrive(copies)
         full[core, z, l, parts[k]] = x_own[parts[k]] + jnp.sum(x_buf[:, parts[k]], axis=0)
         here = full.at[core, z, l, parts[k]]
-        return [wire.start(here, here, beside_y, col)]
+        return wire.start([(here, here, beside_y, col)])
 
     def gather_z(k, copies):
         arrive(copies)
         here = full.at[core, z, :, parts[k]]
-        return [wire.start(here, here, p * 4 + l * 2 + core, col) for p in z_peers]
+        return wire.start(
+            [(here, here, p * 4 + l * 2 + core, col) for p in z_peers],
+            full.at[0, pl.ds(0, max(n_z - 1, 1)), :, parts[k]],
+        )
 
     def gather_cores(k, copies):
         arrive(copies)
         here = full.at[core, :, :, parts[k]]
-        return [wire.start(here, here, sibling, col)]
+        return wire.start([(here, here, sibling, col)])
 
     def couple(i):
         stacked = pb[i].reshape(n_x * n_b, p_size)
         coup[i] = dot(stacked, tr[i], 1, 1).reshape(coup.shape[1:])
         coup_in[x * n_y + i] = coup[i, x]
 
-    def give(i):
-        return [wire.start(coup.at[i, p], coup_in.at[x * n_y + i], scen, p * n_y + y) for p in x_peers]
+    def give(some):
+        return wire.start(
+            [(coup.at[i, p], coup_in.at[x * n_y + i], scen, p * n_y + y) for i in some for p in x_peers],
+            coup.at[pl.ds(0, len(some)), pl.ds(0, n_x - 1)],
+        )
 
     def widen(i):
         high, low = split(coup_in[i], 2)
@@ -288,6 +315,7 @@
         upper[...] = jnp.zeros(upper.shape, F32)
     with jax.named_scope("z0"):
         s0 = add_z(0, s0)
+    far = (y + 2) % n_y
     with jax.named_scope("l0"):
         s0 = add_l(0, s0)
     with jax.named_scope("z1"):
@@ -299,10 +327,9 @@
             h = tr.shape[1] // 2
             up, down = (y + 1) % n_y, (y + n_y - 1) % n_y
             low_half, high_half = tr.at[down, pl.ds(0, h)], tr.at[up, pl.ds(h, h)]
-            far_copies = [
-                wire.start(low_half, low_half, scen, x * n_y + up),
-                wire.start(high_half, high_half, scen, x * n_y + down),
-            ]
+            far_copies = wire.start(
+                [(low_half, low_half, scen, x * n_y + up), (high_half, high_half, scen, x * n_y + down)], tr.at[0]
+            )
         loads[6].wait()
         arrive(pb_copies)
     with jax.named_scope("couple"):
@@ -310,7 +337,7 @@
             couple(i)
     with jax.named_scope("y0"):
         s0 = add_y(0, s0)
-        q_near = [copy for i in [y] + near for copy in give(i)]
+        q_near = give([y] + near)
     with jax.named_scope("l1"):
         s1 = add_l(1, s1)
     with jax.named_scope("x0"):
@@ -323,9 +350,8 @@
         q_far = []
         if n_y == 4:
             arrive(far_copies)
-            far = (y + 2) % n_y
             couple(far)
-            q_far = give(far)
+            q_far = give([far])
     with jax.named_scope("q_near"):
         arrive(q_near)
     with jax.named_scope("widen_near"):
@@ -347,9 +373,9 @@
     with jax.named_scope("total"):
         high, low = split(wide[...], 2)
         total[...] = dot(row_map[...], high, 1, 0) + dot(row_map[...], low, 1, 0)
-        pc_copy = wire.start(total.at[pl.ds((1 - core) * p_rows, p_rows)], pc_buf, sibling, col)
+        pc_copies = wire.start([(total.at[pl.ds((1 - core) * p_rows, p_rows)], pc_buf, sibling, col)])
     with jax.named_scope("drain0"):
-        wire.drain(2 * n_z + 2)
+        wire.drain(4)
     with jax.named_scope("hg0"):
         arrive(s0)
 
@@ -363,18 +389,23 @@
                 block = block + jnp.where(rr == cc, bar_in[:, 128 * r : 128 * r + 128], 0.0)
             work[128 * r : 128 * r + 128, 128 * j : 128 * j + 128] = block
 
+    zero = jnp.broadcast_to(bar_in[:, :128] * 0.0, (8, 128))
+
     def block_step(o):
         with jax.named_scope("block"):
-            u, inv = factor_block(work[pl.ds(o, 128), pl.ds(o, 128)])
+            u, inv = factor_block(work[pl.ds(o, 128), pl.ds(o, 128)], zero)
             upper[pl.ds(o, 128), pl.ds(o, 128)] = u
             inverse[pl.ds(o, 128), :] = inv
         return inv
 
-    def trail(k, inv):
+    def lead_row(k, inv):
+        s = 128 * k
+        upper[s : s + 128, s + 128 :] = dot(inv, work[s : s + 128, s + 128 :], 1, 0, HIGHEST)
+
+    def trail(k):
         with jax.named_scope("trail"):
             s = 128 * k
-            beside = dot(inv, work[s : s + 128, s + 128 :], 1, 0, HIGHEST)
-            upper[s : s + 128, s + 128 :] = beside
+            beside = upper[s : s + 128, s + 128 :]
             for j in range(k + 1, NB):
                 lead = beside[:, 128 * (j - k - 1) : 128 * (j - k)]
                 tail = beside[:, 128 * (j - k - 1) :]
@@ -384,18 +415,22 @@
     inv = block_step(0)
     with jax.named_scope("zg1"):
         s1 = gather_cores(1, s1)
+    with jax.named_scope("pc_wait"):
+        arrive(pc_copies)
+        p_half[...] = total[pl.ds(core * p_rows, p_rows)] + pc_buf[...]
+        pz_copies = wire.start(
+            [
+                (p_half.at[pl.ds(((zy + d) % n_zy) * p_chunk, p_chunk)], pz_buf.at[d - 1], zy_peers[d - 1], col)
+                for d in range(1, n_zy)
+            ],
+            pz_buf,
+        )
     with jax.named_scope("hg1"):
+        lead_row(0, inv)
         arrive(s1)
         for r in range(1, NB):
             load_row(r)
-    trail(0, inv)
-    with jax.named_scope("pc_wait"):
-        pc_copy.wait_recv()
-        p_half[...] = total[pl.ds(core * p_rows, p_rows)] + pc_buf[...]
-        pz_copies = [
-            wire.start(p_half.at[pl.ds(((zy + d) % n_zy) * p_chunk, p_chunk)], pz_buf.at[d - 1], zy_peers[d - 1], col)
-            for d in range(1, n_zy)
-        ]
+    trail(0)
 
     def step(b, carry):
         inv = block_step(pl.multiple_of(b * 128, 128))
@@ -403,7 +438,8 @@
 
             @pl.when(b == k)
             def _():
-                trail(k, inv)
+                lead_row(k, inv)
+                trail(k)
 
         return carry
 
@@ -457,7 +493,7 @@
     cbp = panel_border.shape[2]
     chunk = TILES // 4 // n_z
     p_rows = 32 * n_z
-    n_copies = 96
+    n_copies = 23
     tile = (8, 128)
     vmem = pl.BlockSpec(memory_space=pltpu.VMEM)
     anywhere = pl.BlockSpec(memory_space=pl.ANY)

time: 74.9 us -> 71.3 us (0.952)
  the two profiles are of different devices: /device:TPU:1 before, /device:TPU:49 now
where the time goes in v4:
time: 71.3 us; the launch traced here: 71.2 us
  Pallas kernels  69.9 us (98%)
  between operations  1.28 us (2%)
    pallas_call x1, Pallas kernels, shards(): pl.pallas_call(functools.partial(kernel, n_x, n_y, n_z), name='slab', out...  69.3 us

profile of v4, /device:TPU:49, one launch (start us, length us, event | category | flops | bytes accessed | tf_op | source)
XLA Modules:
  0.0 71.2 jit_solution(12133630173040872166)
XLA Ops:
  1.3 69.3 %slab.1 = (f32[32,512]{1,0:T(8,128)S(1)}, f32[15,512]{1,0:T(8,128)S(1)}) custom-call(s32[1]{0:T(128)S(6)} %copy.9.order_ref, s32[16,256]{1,0:T(8,128)} %columns_ref.1, s32[1,16,48]{2,1,0:T(8,128)} %rows_ref.1, f32[1,512]{1,0:T(1,128)} %bitcast.1, bf16[1,512,512]{2,1,0:T(8,128)(2,1)} %inv_ref.1, bf16[1,256,512]{2,1,0:T(8,128)(2,1)} %border_ref.1, ...), custom_call_target="tpu_custom_call" | custom-call | tf_op jit(solution)/shard_map/slab/pallas_call | solution.py:538
  70.6 0.6 out.1

commit v5 on v4

--- a/solution.py
+++ b/solution.py
@@ -342,28 +342,28 @@
         s1 = add_l(1, s1)
     with jax.named_scope("x0"):
         s0 = add_x(0, s0)
+    with jax.named_scope("y1"):
+        s1 = add_y(1, s1)
     with jax.named_scope("lg0"):
         s0 = gather_z(0, s0)
-    with jax.named_scope("y1"):
-        s1 = add_y(1, s1)
     with jax.named_scope("far"):
         q_far = []
         if n_y == 4:
             arrive(far_copies)
             couple(far)
             q_far = give([far])
+    with jax.named_scope("x1"):
+        s1 = add_x(1, s1)
     with jax.named_scope("q_near"):
         arrive(q_near)
     with jax.named_scope("widen_near"):
         for i in [y] + near:
             for k in range(n_x):
                 widen(k * n_y + i)
-    with jax.named_scope("x1"):
-        s1 = add_x(1, s1)
+    with jax.named_scope("lg1"):
+        s1 = gather_z(1, s1)
     with jax.named_scope("zg0"):
         s0 = gather_cores(0, s0)
-    with jax.named_scope("lg1"):
-        s1 = gather_z(1, s1)
     with jax.named_scope("q_far"):
         arrive(q_far)
     with jax.named_scope("widen_far"):
@@ -375,7 +375,7 @@
         total[...] = dot(row_map[...], high, 1, 0) + dot(row_map[...], low, 1, 0)
         pc_copies = wire.start([(total.at[pl.ds((1 - core) * p_rows, p_rows)], pc_buf, sibling, col)])
     with jax.named_scope("drain0"):
-        wire.drain(4)
+        wire.drain(5)
     with jax.named_scope("hg0"):
         arrive(s0)
 

time: 71.3 us -> 69.4 us (0.973)
  the two profiles are of different devices: /device:TPU:49 before, /device:TPU:1 now
where the time goes in v5:
time: 69.4 us; the launch traced here: 69.3 us
  Pallas kernels  68 us (98%)
  between operations  1.28 us (2%)
    pallas_call x1, Pallas kernels, shards(): pl.pallas_call(functools.partial(kernel, n_x, n_y, n_z), name='slab', out...  67.3 us

profile of v5, /device:TPU:1, one launch (start us, length us, event | category | flops | bytes accessed | tf_op | source)
XLA Modules:
  0.0 69.3 jit_solution(3574441819258462362)
XLA Ops:
  1.3 67.3 %slab.1 = (f32[32,512]{1,0:T(8,128)S(1)}, f32[15,512]{1,0:T(8,128)S(1)}) custom-call(s32[1]{0:T(128)S(6)} %copy.9.order_ref, s32[16,256]{1,0:T(8,128)} %columns_ref.1, s32[1,16,48]{2,1,0:T(8,128)} %rows_ref.1, f32[1,512]{1,0:T(1,128)} %bitcast.1, bf16[1,512,512]{2,1,0:T(8,128)(2,1)} %inv_ref.1, bf16[1,256,512]{2,1,0:T(8,128)(2,1)} %border_ref.1, ...), custom_call_target="tpu_custom_call" | custom-call | tf_op jit(solution)/shard_map/slab/pallas_call | solution.py:538
  68.6 0.6 out.1

commit v6 on v5

--- a/solution.py
+++ b/solution.py
@@ -30,6 +30,13 @@
     return lax.dot_general(
         a, b, (((ca,), (cb,)), ((), ())), precision=precision, preferred_element_type=F32
     )
+
+
+def dot_halves(a, b, ca, cb):
+    rows = a.shape[0]
+    (a_high, a_low), (b_high, b_low) = split(a, 2), split(b, 2)
+    both = dot(jnp.concatenate([a_high, a_low], axis=0), b_high, ca, cb)
+    return both[:rows] + (both[rows:] + dot(a_high, b_low, ca, cb))
 
 
 def one_hot(targets, height):
@@ -456,10 +463,10 @@
         rows = p_half[pl.ds(zy * p_chunk, p_chunk)] + jnp.sum(pz_buf[...], axis=0)
         solved = []
         for b in range(NB):
-            done = dot(rows[:, :128], inverse[128 * b : 128 * b + 128, :], 1, 1, HIGHEST)
+            done = dot_halves(rows[:, :128], inverse[128 * b : 128 * b + 128, :], 1, 1)
             solved.append(done)
             if b < NB - 1:
-                rows = rows[:, 128:] - dot(done, upper[128 * b : 128 * b + 128, 128 * b + 128 :], 1, 0, HIGHEST)
+                rows = rows[:, 128:] - dot_halves(done, upper[128 * b : 128 * b + 128, 128 * b + 128 :], 1, 0)
         slab_ref[...] = jnp.concatenate(solved, axis=1)[: slab_ref.shape[0]]
     with jax.named_scope("drain1"):
         wire.drain()
@@ -496,7 +503,6 @@
     n_copies = 23
     tile = (8, 128)
     vmem = pl.BlockSpec(memory_space=pltpu.VMEM)
-    anywhere = pl.BlockSpec(memory_space=pl.ANY)
     scratch = [
         pltpu.SMEM((1,), jnp.int32),
         pltpu.VMEM(slab_columns.shape, jnp.int32),
@@ -541,7 +547,7 @@
         out_shape=tuple(
             pltpu.VMEM(shape, F32) for shape in ((DIAG // n_col, DIAG), (15, DIAG))
         ),
-        in_specs=[anywhere] * 7,
+        in_specs=[pl.BlockSpec(memory_space=pltpu.HBM)] * 7,
         out_specs=[vmem] * 2,
         scratch_shapes=scratch,
         compiler_params=pltpu.CompilerParams(collective_id=0, has_side_effects=True),

time: 69.4 us -> 68.6 us (0.988)
  Pallas kernels: 68 us -> 67.2 us
    pallas_call x1, Pallas kernels: 67.3 us -> 66.6 us  [shards(): pl.pallas_call(functools.partial(kernel, n_x, n_y, n_z), name='slab', out...]
where the time goes in v6:
time: 68.6 us; the launch traced here: 68.5 us
  Pallas kernels  67.2 us (98%)
  between operations  1.28 us (2%)
    pallas_call x1, Pallas kernels, shards(): pl.pallas_call(functools.partial(kernel, n_x, n_y, n_z), name='slab', out...  66.6 us

profile of v6, /device:TPU:1, one launch (start us, length us, event | category | flops | bytes accessed | tf_op | source)
XLA Modules:
  0.0 68.5 jit_solution(5663696542446267901)
XLA Ops:
  1.3 66.6 %slab.1 = (f32[32,512]{1,0:T(8,128)S(1)}, f32[15,512]{1,0:T(8,128)S(1)}) custom-call(s32[1]{0:T(128)S(6)} %copy.9.order_ref, s32[16,256]{1,0:T(8,128)} %columns_ref.1, s32[1,16,48]{2,1,0:T(8,128)} %rows_ref.1, f32[1,512]{1,0:T(1,128)} %bitcast.1, bf16[1,512,512]{2,1,0:T(8,128)(2,1)} %inv_ref.1, bf16[1,256,512]{2,1,0:T(8,128)(2,1)} %border_ref.1, ...), custom_call_target="tpu_custom_call" | custom-call | tf_op jit(solution)/shard_map/slab/pallas_call | solution.py:544
  67.9 0.6 out.1
